TPU v7x, 32 devices: a whole 2x2x4 slice. The times are simulated.
32 devices in a mesh: groups: 2 (over y), block: 16 (over z, x, core).
Axes of the slice: x: 2, y: 2, z: 4, core: 2. Of those that a mesh axis runs over, the one named last changes fastest.
Arguments:
- queries: bfloat16 [49152, 1024], P(('groups', 'block')), parts along dimension 0, may hold values from -6 to 6
- keys: bfloat16 [49152, 1024], P(('groups', 'block')), parts along dimension 0, may hold values from -16 to 16
- values: bfloat16 [49152, 1024], P(('groups', 'block')), parts along dimension 0, may hold values from -12 to 12
Outputs:
- attended: bfloat16 [49152, 1024], P(('groups', 'block')), parts along dimension 0
There are 2 independent parts, one for each index of `groups`. A program takes and returns all parts, laid end to end along the dimension named above; each array names one. Nothing has to cross between parts.
All inputs are finite; a program needn't handle non-finite values.
Results may differ from a plain program's by a relative error of at most 0.0029.
Values sent between devices are 32-bit elements; how exact they have to be, the bound alone decides.
No kernel may reach another device: no remote copies, remote signals or barrier semaphores. Data moves between devices by JAX's collectives and lax.ppermute only.
A program may use at most 128 MiB of HBM per device.

v0:
```python
import functools

import jax
import jax.numpy as jnp
from jax import lax
from jax.experimental import pallas as pl
from jax.experimental.pallas import tpu as pltpu
from jax.sharding import PartitionSpec as P


HEADS = 8
HEAD_DIM = 128
SPAN = 128
HALF = HEADS // 2
PIECE = HEAD_DIM + 8
OFFSETS = ((0, 1, 2, 3), (0, 2, 3, 1))

VM = pl.BlockSpec(memory_space=pltpu.VMEM)
HBM = pl.BlockSpec(memory_space=pltpu.HBM)


def place():
    me = lax.axis_index("block")
    return me & 1, (me >> 1) & 3, me >> 3


def offset_of(core, slot):
    return jnp.where(core == 0, OFFSETS[0][slot], OFFSETS[1][slot])


def head_columns(mine, slot):
    core, local, _ = place()
    core = core if mine else 1 - core
    head = core * HALF + (offset_of(core, slot) ^ local)
    return pl.ds(pl.multiple_of(head * HEAD_DIM, HEAD_DIM), HEAD_DIM)


def features(x):
    x = x.astype(jnp.float32)
    return jnp.where(x > 0, x + 1.0, jnp.exp(x)).astype(jnp.bfloat16)


def key_states(count, k_ref, v_ref, fk_ref, pf_ref, nf_ref, t_ref):
    acc = jnp.zeros((HEAD_DIM, HEAD_DIM), jnp.float32)
    norm = jnp.zeros((1, HEAD_DIM), jnp.float32)
    for c in range(count):
        rows = pl.ds(c * SPAN, SPAN)
        fk = features(k_ref[rows, :])
        fk_ref[rows, :] = fk
        pf_ref[rows, :] = acc
        nf_ref[pl.ds(c, 1), :] = norm
        acc = acc + lax.dot_general(
            fk, v_ref[rows, :], (((0,), (0,)), ((), ())), preferred_element_type=jnp.float32
        )
        norm = norm + jnp.sum(fk.astype(jnp.float32), axis=0, keepdims=True)
    t_ref[pl.ds(0, HEAD_DIM), :] = acc
    t_ref[pl.ds(HEAD_DIM, 8), :] = jnp.broadcast_to(norm, (8, HEAD_DIM))


def pre_a(count, k_hbm, v_hbm, k_ref, v_ref, fk_ref, pf_ref, nf_ref, t_ref, sems):
    copies = []
    for j in range(HEADS):
        cols = head_columns(j >= HALF, j % HALF)
        ck = pltpu.make_async_copy(k_hbm.at[:, cols], k_ref.at[j], sems.at[0, j])
        cv = pltpu.make_async_copy(v_hbm.at[:, cols], v_ref.at[j], sems.at[1, j])
        ck.start()
        cv.start()
        copies.append((ck, cv))
    for j in range(HALF):
        copies[j][0].wait()
        copies[j][1].wait()
        key_states(
            count, k_ref.at[j], v_ref.at[j], fk_ref.at[j], pf_ref.at[j], nf_ref.at[j], t_ref.at[j]
        )
    for j in range(HALF, HEADS):
        copies[j][0].wait()
        copies[j][1].wait()


def pre_b(count, k_ref, v_ref, fk_ref, pf_ref, nf_ref, t_ref):
    for s in range(HALF):
        key_states(
            count,
            k_ref.at[HALF + s],
            v_ref.at[HALF + s],
            fk_ref.at[s],
            pf_ref.at[s],
            nf_ref.at[s],
            t_ref.at[s],
        )


def mid(count, mine, q_ref, fk_ref, nf_ref, fqs_ref, den_ref):
    causal = lax.broadcasted_iota(jnp.int32, (SPAN, SPAN), 0) >= lax.broadcasted_iota(
        jnp.int32, (SPAN, SPAN), 1
    )
    for s in range(HALF):
        cols = head_columns(mine, s)
        for c in range(count):
            rows = pl.ds(c * SPAN, SPAN)
            fq = features(q_ref[rows, cols])
            scores = lax.dot_general(
                fq, fk_ref[s, rows, :], (((1,), (1,)), ((), ())), preferred_element_type=jnp.float32
            )
            scores = jnp.where(causal, scores, 0.0)
            den = jnp.sum(
                scores + fq.astype(jnp.float32) * nf_ref[s, pl.ds(c, 1), :], axis=-1, keepdims=True
            )
            fqs_ref[s, rows, pl.ds(0, HEAD_DIM)] = fq
            fqs_ref[s, rows, pl.ds(HEAD_DIM, SPAN)] = scores.astype(jnp.bfloat16)
            den_ref[s, rows, :] = jnp.broadcast_to(den, (SPAN, HEAD_DIM))


def post(count, mine, slots, fqs_ref, den_ref, pf_ref, v_ref, b_ref, *rest):
    o_hbm, done_ref, o_ref, sems = rest[-4:]
    done_ref[...] = jnp.zeros_like(done_ref)
    first = HALF if mine else 0
    copies = []
    for i, s in enumerate(slots):
        before = b_ref[i, pl.ds(0, HEAD_DIM), :]
        before_norm = b_ref[i, pl.ds(HEAD_DIM, 1), :]
        for c in range(count):
            rows = pl.ds(c * SPAN, SPAN)
            fqs = fqs_ref[s, rows, :]
            prior = (pf_ref[s, rows, :] + before).astype(jnp.bfloat16)
            num = jnp.dot(
                fqs,
                jnp.concatenate([prior, v_ref[first + s, rows, :]], axis=0),
                preferred_element_type=jnp.float32,
            )
            fq = fqs[:, :HEAD_DIM].astype(jnp.float32)
            den = den_ref[s, rows, :] + jnp.sum(fq * before_norm, axis=-1, keepdims=True)
            o_ref[i, rows, :] = (num / den).astype(jnp.bfloat16)
        copy = pltpu.make_async_copy(o_ref.at[i], o_hbm.at[:, head_columns(mine, s)], sems.at[i])
        copy.start()
        copies.append(copy)
    for copy in copies:
        copy.wait()


def add_totals(keep_ref, got_ref, *piece_refs):
    for s in range(HALF):
        piece_refs[s][...] = keep_ref[s] + got_ref[s]


def inside_group(p0, p1, p2, p3, tied, e0, e1, e2, e3, total_ref):
    core, local, _ = place()
    pieces = [p[...] for p in (p0, p1, p2, p3)]
    chips = [local ^ offset_of(core, s) for s in range(4)]
    for s, e in enumerate((e0, e1, e2, e3)):
        acc = jnp.zeros((PIECE, HEAD_DIM), jnp.float32)
        for o in range(4):
            if o != s:
                acc = acc + jnp.where(chips[o] < chips[s], pieces[o], 0.0)
        e[...] = acc
    total_ref[...] = (pieces[0] + pieces[1]) + (pieces[2] + pieces[3])


def across_groups(bit, e0, e1, e2, e3, total_ref, got_ref, tied, f0, f1, f2, f3, sum_ref):
    _, _, group = place()
    got = got_ref[...]
    earlier = jnp.where((group & bit) != 0, got, 0.0)
    for e, f in zip((e0, e1, e2, e3), (f0, f1, f2, f3)):
        f[...] = e[...] + earlier
    sum_ref[...] = total_ref[...] + got


def both_cores(slots, *refs):
    n = len(slots)
    keep_ref, got_ref = refs[n : n + 2]
    mine_ref, send_ref = refs[-2:]
    core, _, _ = place()
    for i, s in enumerate(slots):
        before = refs[i][...]
        mine_ref[i] = before + jnp.where(core == 1, got_ref[s], 0.0)
        send_ref[i] = before + jnp.where(core == 0, keep_ref[s], 0.0)


def per_device(queries, keys, values):
    rows = queries.shape[0]
    count = rows // SPAN
    devices_n = lax.axis_size("block")
    groups_n = devices_n // 8
    assert groups_n * 8 == devices_n and groups_n & (groups_n - 1) == 0

    f32, bf16 = jnp.float32, jnp.bfloat16
    sds = jax.ShapeDtypeStruct
    state_shapes = (
        sds((HALF, rows, HEAD_DIM), bf16),
        sds((HALF, rows, HEAD_DIM), f32),
        sds((HALF, (count + 7) // 8 * 8, HEAD_DIM), f32),
        sds((HALF, PIECE, HEAD_DIM), f32),
    )
    half_flops = HALF * count * 2 * SPAN * HEAD_DIM * HEAD_DIM

    def call(kernel, ins, outs, in_specs=None, out_specs=None, grant=8, flops=half_flops, nbytes=8 << 20, **more):
        return pl.pallas_call(
            kernel,
            out_shape=outs,
            in_specs=in_specs or [VM] * len(ins),
            out_specs=out_specs or (VM,) * len(outs),
            compiler_params=pltpu.CompilerParams(vmem_limit_bytes=grant << 20),
            cost_estimate=pl.CostEstimate(flops=flops, bytes_accessed=nbytes, transcendentals=0),
            **more,
        )(*ins)

    def small(kernel, ins, outs):
        return call(kernel, ins, outs, flops=1 << 20, nbytes=1 << 19)

    def swap(x, distance):
        return lax.ppermute(x, "block", [(i, i ^ distance) for i in range(devices_n)])

    def swap_slot(x, slot):
        return lax.ppermute(
            x, "block", [(i, i ^ (2 * OFFSETS[i & 1][slot])) for i in range(devices_n)]
        )

    k_vm, v_vm, fk_a, pf_a, nf_a, t_send = call(
        functools.partial(pre_a, count),
        (keys, values),
        (sds((HEADS, rows, HEAD_DIM), bf16),) * 2 + state_shapes,
        in_specs=[HBM, HBM],
        grant=42,
        scratch_shapes=[pltpu.SemaphoreType.DMA((2, HEADS))],
    )
    t_got = swap(t_send, 1)
    fk_b, pf_b, nf_b, t_keep = call(functools.partial(pre_b, count), (k_vm, v_vm), state_shapes)

    def mid_call(mine, fk, nf):
        return call(
            functools.partial(mid, count, mine),
            (queries, fk, nf),
            (sds((HALF, rows, 2 * HEAD_DIM), bf16), sds((HALF, rows, HEAD_DIM), f32)),
        )

    piece = sds((PIECE, HEAD_DIM), f32)

    pieces = small(add_totals, (t_keep, t_got), (piece,) * 4)
    landed = {s: swap_slot(pieces[s], s) for s in (2, 3, 1)}
    fqs_b, den_b = mid_call(True, fk_b, nf_b)
    *finals, total = small(
        inside_group, (pieces[0], landed[1], landed[2], landed[3], den_b), (piece,) * 5
    )
    fqs_a, den_a = mid_call(False, fk_a, nf_a)
    bit = 1
    while bit < groups_n:
        got = swap(total, 8 * bit)
        *finals, total = small(
            functools.partial(across_groups, bit), (*finals, total, got, den_a), (piece,) * 5
        )
        bit *= 2
    back = {0: finals[0]}
    for s in (2, 3, 1):
        back[s] = swap_slot(finals[s], s)

    out = done = None
    for slots in ((0, 2), (3, 1)):
        two = sds((len(slots), PIECE, HEAD_DIM), f32)
        before_b, send_a = small(
            functools.partial(both_cores, slots),
            (*[back[s] for s in slots], t_keep, t_got, *([] if done is None else [done])),
            (two, two),
        )
        before_a = swap(send_a, 1)
        for mine, fqs, den, pf, b in (
            (True, fqs_b, den_b, pf_b, before_b),
            (False, fqs_a, den_a, pf_a, before_a),
        ):
            extra = () if out is None else (out,)
            out, done = call(
                functools.partial(post, count, mine, slots),
                (fqs, den, pf, v_vm, b, *extra),
                (sds((rows, HEADS * HEAD_DIM), bf16), sds((8, HEAD_DIM), f32)),
                in_specs=[VM] * 5 + [HBM] * len(extra),
                out_specs=(HBM, VM),
                scratch_shapes=[
                    pltpu.VMEM((len(slots), rows, HEAD_DIM), bf16),
                    pltpu.SemaphoreType.DMA((len(slots),)),
                ],
                input_output_aliases={5: 0} if extra else {},
            )
    return out


def solution(mesh):
    placed = P(("groups", "block"), None)

    return jax.shard_map(
        per_device,
        mesh=mesh,
        in_specs=(placed, placed, placed),
        out_specs=placed,
        check_vma=False,
    )
```

profile of v0, /device:TPU:0, one launch (start us, length us, event | category | flops | bytes accessed | tf_op | source)
XLA Modules:
  0.0 35.8 jit_solution(7306732008070667210)
XLA Ops:
  0.0 3.1 %shard_map.37 = (bf16[8,1536,128]{2,1,0:T(8,128)(2,1)S(1)}, bf16[8,1536,128]{2,1,0:T(8,128)(2,1)S(1)}, bf16[4,1536,128]{2,1,0:T(8,128)(2,1)S(1)}, f32[4,1536,128...) custom-call(bf16[1536,1024]{1,0:T(8,128)(2,1)} %k_hbm.1, bf16[1536,1024]{1,0:T(8,128)(2,1)} %v_hbm.1), custom_call_target="tpu_custom_call" | custom-call | flops 201326592 | bytes 8388608 | tf_op jit(solution)/shard_map/pallas_call | solution.py:197
  3.1 0.6 %collective-permute-start = (f32[4,136,128]{2,1,0:T(8,128)S(1)}, f32[4,136,128]{2,1,0:T(8,128)S(1)}, u32[]{:S(2)}, u32[]{:S(2)}) collective-permute-start(f32[4,136,128]{2,1,0:T(8,128)S(1)} %get-tuple-element.49), channel_id=1, source_target_pairs={{0,1},{1,0},{2,3},{3,2},{4,5},{5,4},{6,7},{7,6},{8,9},{9,8},{10,11... | collective-permute-start | bytes 835592 | tf_op jit(solution)/shard_map/ppermute | solution.py:211
  3.7 0.0 copy-start
  3.7 1.3 %shard_map.39 = (bf16[4,1536,128]{2,1,0:T(8,128)(2,1)S(1)}, f32[4,1536,128]{2,1,0:T(8,128)S(1)}, f32[4,16,128]{2,1,0:T(8,128)S(1)}, f32[4,136,128]{2,1,0:T(8,128)S(1)}) custom-call(bf16[8,1536,128]{2,1,0:T(8,128)(2,1)S(1)} %get-tuple-element.47.k_ref, bf16[8,1536,128]{2,1,0:T(8,128)(2,1)S(1)} %get-tuple-element.46.v_ref), custom_call_target="tpu_custom_call" | custom-call | flops 201326592 | bytes 8388608 | tf_op jit(solution)/shard_map/pallas_call | solution.py:197
  5.0 0.0 collective-permute-done.got_ref.refs_3_
  5.0 2.8 %collective-permute-start.1 = (f32[136,128]{1,0:T(8,128)S(1)}, f32[136,128]{1,0:T(8,128)S(1)}, u32[]{:S(2)}, u32[]{:S(2)}) collective-permute-start(f32[136,128]{1,0:T(8,128)S(1)} %get-tuple-element.51), channel_id=1, source_target_pairs={{0,2},{1,5},{2,0},{3,7},{4,6},{5,1},{6,4},{7,3},{8,10},{9,13},{10,... | collective-permute-start | bytes 208904 | tf_op jit(solution)/shard_map/ppermute | solution.py:214
  7.8 1.6 %collective-permute-start.2 = (f32[136,128]{1,0:T(8,128)S(1)}, f32[136,128]{1,0:T(8,128)S(1)}, u32[]{:S(2)}, u32[]{:S(2)}) collective-permute-start(f32[136,128]{1,0:T(8,128)S(1)} %get-tuple-element.52), channel_id=1, source_target_pairs={{0,4},{1,7},{2,6},{3,5},{4,0},{5,3},{6,2},{7,1},{8,12},{9,15},{10,... | collective-permute-start | bytes 208904 | tf_op jit(solution)/shard_map/ppermute | solution.py:214
  9.4 0.0 collective-permute-start.3
  9.4 0.0 copy-done
  9.4 1.5 %shard_map.41 = (bf16[4,1536,256]{2,1,0:T(8,128)(2,1)S(1)}, f32[4,1536,128]{2,1,0:T(8,128)S(1)}) custom-call(bf16[1536,1024]{1,0:T(8,128)(2,1)S(1)} %copy-done, bf16[4,1536,128]{2,1,0:T(8,128)(2,1)S(1)} %get-tuple-element.54.fk_ref, f32[4,16,128]{2,1,0:T(8,128)S(1)} %get-tuple-element.55.nf_ref), custom_call_target="tpu_custom_call" | custom-call | flops 201326592 | bytes 8388608 | tf_op jit(solution)/shard_map/pallas_call | solution.py:197
  10.9 0.0 collective-permute-done.1.p1
  10.9 1.9 %collective-permute-done.2.p2 = f32[136,128]{1,0:T(8,128)S(1)} collective-permute-done((f32[136,128]{1,0:T(8,128)S(1)}, f32[136,128]{1,0:T(8,128)S(1)}, u32[]{:S(2)}, u32[]{:S(2)}) %collective-permute-start.2) | collective-permute-done | bytes 69664 | tf_op jit(solution)/shard_map/ppermute | solution.py:214
  12.8 1.8 %collective-permute-done.3.p3 = f32[136,128]{1,0:T(8,128)S(1)} collective-permute-done((f32[136,128]{1,0:T(8,128)S(1)}, f32[136,128]{1,0:T(8,128)S(1)}, u32[]{:S(2)}, u32[]{:S(2)}) %collective-permute-start.3) | collective-permute-done | bytes 69664 | tf_op jit(solution)/shard_map/ppermute | solution.py:214
  14.6 0.1 shard_map.42
  14.7 2.7 %collective-permute-start.4 = (f32[136,128]{1,0:T(8,128)S(1)}, f32[136,128]{1,0:T(8,128)S(1)}, u32[]{:S(2)}, u32[]{:S(2)}) collective-permute-start(f32[136,128]{1,0:T(8,128)S(1)} %get-tuple-element.61.total_ref), channel_id=1, source_target_pairs={{0,8},{1,9},{2,10},{3,11},{4,12},{5,13},{6,14},{7,15},{8,0},{9,1},... | collective-permute-start | bytes 208904 | tf_op jit(solution)/shard_map/ppermute | solution.py:211
  17.3 1.5 %shard_map.38 = (bf16[4,1536,256]{2,1,0:T(8,128)(2,1)S(1)}, f32[4,1536,128]{2,1,0:T(8,128)S(1)}) custom-call(bf16[1536,1024]{1,0:T(8,128)(2,1)S(1)} %copy-done, bf16[4,1536,128]{2,1,0:T(8,128)(2,1)S(1)} %get-tuple-element.41.fk_ref, f32[4,16,128]{2,1,0:T(8,128)S(1)} %get-tuple-element.42.nf_ref), custom_call_target="tpu_custom_call" | custom-call | flops 201326592 | bytes 8388608 | tf_op jit(solution)/shard_map/pallas_call | solution.py:197
  18.8 1.7 %collective-permute-done.4.got_ref = f32[136,128]{1,0:T(8,128)S(1)} collective-permute-done((f32[136,128]{1,0:T(8,128)S(1)}, f32[136,128]{1,0:T(8,128)S(1)}, u32[]{:S(2)}, u32[]{:S(2)}) %collective-permute-start.4) | collective-permute-done | bytes 69664 | tf_op jit(solution)/shard_map/ppermute | solution.py:211
  20.6 0.7 %shard_map.43 = (f32[136,128]{1,0:T(8,128)S(1)}, f32[136,128]{1,0:T(8,128)S(1)}, f32[136,128]{1,0:T(8,128)S(1)}, f32[136,128]{1,0:T(8,128)S(1)}, f32[136,128]{1,0:T(8,128)}) custom-call(f32[136,128]{1,0:T(8,128)S(1)} %get-tuple-element.57.e0, f32[136,128]{1,0:T(8,128)S(1)} %get-tuple-element.58.e1, f32[136,128]{1,0:T(8,128)S(1)} %get-tuple-element.59.e2, ...), custom_call_target="tpu_custom_call" | custom-call | flops 1048576 | bytes 524288 | tf_op jit(solution)/shard_map/pallas_call | solution.py:197
  21.2 0.0 collective-permute-start.7
  21.2 4.3 %collective-permute-done.7.refs_1_ = f32[136,128]{1,0:T(8,128)S(1)} collective-permute-done((f32[136,128]{1,0:T(8,128)S(1)}, f32[136,128]{1,0:T(8,128)S(1)}, u32[]{:S(2)}, u32[]{:S(2)}) %collective-permute-start.7) | collective-permute-done | bytes 69664 | tf_op jit(solution)/shard_map/ppermute | solution.py:214
  25.6 0.1 collective-permute-start.8
  25.6 0.3 collective-permute-start.5
  26.0 1.2 %collective-permute-start.6 = (f32[136,128]{1,0:T(8,128)S(1)}, f32[136,128]{1,0:T(8,128)S(1)}, u32[]{:S(2)}, u32[]{:S(2)}) collective-permute-start(f32[136,128]{1,0:T(8,128)S(1)} %get-tuple-element.63), channel_id=1, source_target_pairs={{0,2},{1,5},{2,0},{3,7},{4,6},{5,1},{6,4},{7,3},{8,10},{9,13},{10,... | collective-permute-start | bytes 208904 | tf_op jit(solution)/shard_map/ppermute | solution.py:214
  27.2 2.1 %shard_map.45 = (bf16[1536,1024]{1,0:T(8,128)(2,1)}, f32[8,128]{1,0:T(8,128)}) custom-call(bf16[4,1536,256]{2,1,0:T(8,128)(2,1)S(1)} %get-tuple-element.67.fqs_ref, f32[4,1536,128]{2,1,0:T(8,128)S(1)} %get-tuple-element.56.tied.den_ref, f32[4,1536,128]{2,1,0:T(8,128)S(1)} %get-tuple-element.68.pf_ref, bf16[8,1536,128]{2,1,0:T(8,128)(2,1)S(1)} %get-tuple-element.46.v_ref, ...), custom_call_target="tpu_custom_call" | custom-call | flops 201326592 | bytes 8388608 | tf_op jit(solution)/shard_map/pallas_call | solution.py:197
  29.3 0.0 collective-permute-done.8.b_ref
  29.3 1.5 %shard_map.46 = (bf16[1536,1024]{1,0:T(8,128)(2,1)}, f32[8,128]{1,0:T(8,128)S(1)}) custom-call(bf16[4,1536,256]{2,1,0:T(8,128)(2,1)S(1)} %get-tuple-element.43.fqs_ref, f32[4,1536,128]{2,1,0:T(8,128)S(1)} %get-tuple-element.44.tied.den_ref, f32[4,1536,128]{2,1,0:T(8,128)S(1)} %get-tuple-element.45.pf_ref, ...), custom_call_target="tpu_custom_call", output_to_operand_aliasing={{0}: (5, {})} | custom-call | flops 201326592 | bytes 8388608 | tf_op jit(solution)/shard_map/pallas_call | solution.py:197
  30.8 0.6 %collective-permute-done.5.refs_0_ = f32[136,128]{1,0:T(8,128)S(1)} collective-permute-done((f32[136,128]{1,0:T(8,128)S(1)}, f32[136,128]{1,0:T(8,128)S(1)}, u32[]{:S(2)}, u32[]{:S(2)}) %collective-permute-start.5) | collective-permute-done | bytes 69664 | tf_op jit(solution)/shard_map/ppermute | solution.py:214
  31.4 0.0 collective-permute-done.6.refs_1_
  31.5 0.1 collective-permute-start.9
  31.5 2.1 %shard_map.48 = (bf16[1536,1024]{1,0:T(8,128)(2,1)}, f32[8,128]{1,0:T(8,128)}) custom-call(bf16[4,1536,256]{2,1,0:T(8,128)(2,1)S(1)} %get-tuple-element.67.fqs_ref, f32[4,1536,128]{2,1,0:T(8,128)S(1)} %get-tuple-element.56.tied.den_ref, f32[4,1536,128]{2,1,0:T(8,128)S(1)} %get-tuple-element.68.pf_ref, ...), custom_call_target="tpu_custom_call", output_to_operand_aliasing={{0}: (5, {})} | custom-call | flops 201326592 | bytes 8388608 | tf_op jit(solution)/shard_map/pallas_call | solution.py:197
  33.7 0.0 collective-permute-done.9.b_ref
  33.7 2.1 %shard_map.49 = (bf16[1536,1024]{1,0:T(8,128)(2,1)}, f32[8,128]{1,0:T(8,128)}) custom-call(bf16[4,1536,256]{2,1,0:T(8,128)(2,1)S(1)} %get-tuple-element.43.fqs_ref, f32[4,1536,128]{2,1,0:T(8,128)S(1)} %get-tuple-element.44.tied.den_ref, f32[4,1536,128]{2,1,0:T(8,128)S(1)} %get-tuple-element.45.pf_ref, ...), custom_call_target="tpu_custom_call", output_to_operand_aliasing={{0}: (5, {})} | custom-call | flops 201326592 | bytes 8388608 | tf_op jit(solution)/shard_map/pallas_call | solution.py:197
  (3 shorter events, 0.1 us)
Async XLA Ops:
  3.1 1.9 %collective-permute-start = (f32[4,136,128]{2,1,0:T(8,128)S(1)}, f32[4,136,128]{2,1,0:T(8,128)S(1)}, u32[]{:S(2)}, u32[]{:S(2)}) collective-permute-start(f32[4,136,128]{2,1,0:T(8,128)S(1)} %get-tuple-element.49), channel_id=1, source_target_pairs={{0,1},{1,0},{2,3},{3,2},{4,5},{5,4},{6,7},{7,6},{8,9},{9,8},{10,11... | collective-permute-start | bytes 835592 | tf_op jit(solution)/shard_map/ppermute | solution.py:211
  3.7 5.7 %copy-start = (bf16[1536,1024]{1,0:T(8,128)(2,1)S(1)}, bf16[1536,1024]{1,0:T(8,128)(2,1)}, u32[]{:S(2)}) copy-start(bf16[1536,1024]{1,0:T(8,128)(2,1)} %q_ref.3) | copy-start | bytes 9437188
  5.0 5.9 %collective-permute-start.1 = (f32[136,128]{1,0:T(8,128)S(1)}, f32[136,128]{1,0:T(8,128)S(1)}, u32[]{:S(2)}, u32[]{:S(2)}) collective-permute-start(f32[136,128]{1,0:T(8,128)S(1)} %get-tuple-element.51), channel_id=1, source_target_pairs={{0,2},{1,5},{2,0},{3,7},{4,6},{5,1},{6,4},{7,3},{8,10},{9,13},{10,... | collective-permute-start | bytes 208904 | tf_op jit(solution)/shard_map/ppermute | solution.py:214
  7.8 5.0 %collective-permute-start.2 = (f32[136,128]{1,0:T(8,128)S(1)}, f32[136,128]{1,0:T(8,128)S(1)}, u32[]{:S(2)}, u32[]{:S(2)}) collective-permute-start(f32[136,128]{1,0:T(8,128)S(1)} %get-tuple-element.52), channel_id=1, source_target_pairs={{0,4},{1,7},{2,6},{3,5},{4,0},{5,3},{6,2},{7,1},{8,12},{9,15},{10,... | collective-permute-start | bytes 208904 | tf_op jit(solution)/shard_map/ppermute | solution.py:214
  9.4 5.2 %collective-permute-start.3 = (f32[136,128]{1,0:T(8,128)S(1)}, f32[136,128]{1,0:T(8,128)S(1)}, u32[]{:S(2)}, u32[]{:S(2)}) collective-permute-start(f32[136,128]{1,0:T(8,128)S(1)} %get-tuple-element.53), channel_id=1, source_target_pairs={{0,6},{1,3},{2,4},{3,1},{4,2},{5,7},{6,0},{7,5},{8,14},{9,11},{10,... | collective-permute-start | bytes 208904 | tf_op jit(solution)/shard_map/ppermute | solution.py:214
  14.7 5.9 %collective-permute-start.4 = (f32[136,128]{1,0:T(8,128)S(1)}, f32[136,128]{1,0:T(8,128)S(1)}, u32[]{:S(2)}, u32[]{:S(2)}) collective-permute-start(f32[136,128]{1,0:T(8,128)S(1)} %get-tuple-element.61.total_ref), channel_id=1, source_target_pairs={{0,8},{1,9},{2,10},{3,11},{4,12},{5,13},{6,14},{7,15},{8,0},{9,1},... | collective-permute-start | bytes 208904 | tf_op jit(solution)/shard_map/ppermute | solution.py:211
  21.2 4.3 %collective-permute-start.7 = (f32[136,128]{1,0:T(8,128)S(1)}, f32[136,128]{1,0:T(8,128)S(1)}, u32[]{:S(2)}, u32[]{:S(2)}) collective-permute-start(f32[136,128]{1,0:T(8,128)S(1)} %get-tuple-element.65), channel_id=1, source_target_pairs={{0,4},{1,7},{2,6},{3,5},{4,0},{5,3},{6,2},{7,1},{8,12},{9,15},{10,... | collective-permute-start | bytes 208904 | tf_op jit(solution)/shard_map/ppermute | solution.py:214
  25.6 3.8 %collective-permute-start.8 = (f32[2,136,128]{2,1,0:T(8,128)S(1)}, f32[2,136,128]{2,1,0:T(8,128)S(1)}, u32[]{:S(2)}, u32[]{:S(2)}) collective-permute-start(f32[2,136,128]{2,1,0:T(8,128)S(1)} %get-tuple-element.66), channel_id=1, source_target_pairs={{0,1},{1,0},{2,3},{3,2},{4,5},{5,4},{6,7},{7,6},{8,9},{9,8},{10,11... | collective-permute-start | bytes 417800 | tf_op jit(solution)/shard_map/ppermute | solution.py:211
  25.6 5.8 %collective-permute-start.5 = (f32[136,128]{1,0:T(8,128)S(1)}, f32[136,128]{1,0:T(8,128)S(1)}, u32[]{:S(2)}, u32[]{:S(2)}) collective-permute-start(f32[136,128]{1,0:T(8,128)S(1)} %get-tuple-element.62), channel_id=1, source_target_pairs={{0,6},{1,3},{2,4},{3,1},{4,2},{5,7},{6,0},{7,5},{8,14},{9,11},{10,... | collective-permute-start | bytes 208904 | tf_op jit(solution)/shard_map/ppermute | solution.py:214
  26.0 5.5 %collective-permute-start.6 = (f32[136,128]{1,0:T(8,128)S(1)}, f32[136,128]{1,0:T(8,128)S(1)}, u32[]{:S(2)}, u32[]{:S(2)}) collective-permute-start(f32[136,128]{1,0:T(8,128)S(1)} %get-tuple-element.63), channel_id=1, source_target_pairs={{0,2},{1,5},{2,0},{3,7},{4,6},{5,1},{6,4},{7,3},{8,10},{9,13},{10,... | collective-permute-start | bytes 208904 | tf_op jit(solution)/shard_map/ppermute | solution.py:214
  31.5 2.2 %collective-permute-start.9 = (f32[2,136,128]{2,1,0:T(8,128)S(1)}, f32[2,136,128]{2,1,0:T(8,128)S(1)}, u32[]{:S(2)}, u32[]{:S(2)}) collective-permute-start(f32[2,136,128]{2,1,0:T(8,128)S(1)} %get-tuple-element.72), channel_id=1, source_target_pairs={{0,1},{1,0},{2,3},{3,2},{4,5},{5,4},{6,7},{7,6},{8,9},{9,8},{10,11... | collective-permute-start | bytes 417800 | tf_op jit(solution)/shard_map/ppermute | solution.py:211
where the time goes:
time: 35.9 us; the launch traced here: 35.8 us
  Pallas kernels  16.1 us (45%)
  waiting for transfers between devices  10.3 us (29%)
  starting transfers between devices  9.24 us (26%)
    pallas_call x13, Pallas kernels, call(): pl.pallas_call(kernel, out_shape=outs, in_specs=in_specs or [VM] * len(in...  16.1 us
    ppermute x6, waiting for transfers between devices, swap_slot(): lax.ppermute(x, 'block', [(i, i ^ 2 * OFFSETS[i & 1][slot]) for i in rang...  8.55 us
    ppermute x6, starting transfers between devices, swap_slot(): lax.ppermute(x, 'block', [(i, i ^ 2 * OFFSETS[i & 1][slot]) for i in rang...  5.88 us
    ppermute x4, starting transfers between devices, swap(): lax.ppermute(x, 'block', [(i, i ^ distance) for i in range(devices_n)])  3.36 us
    ppermute x4, waiting for transfers between devices, swap(): lax.ppermute(x, 'block', [(i, i ^ distance) for i in range(devices_n)])  1.73 us
  transfers between devices with their start and end apart: 10, of which 5 were waited for; matrix products, arithmetic and copies ran while one was open for 0% of the time, Pallas kernels for 28%

commit v1 on v0

v1 whole, which is shorter than its diff:
```python
import functools

import jax
import jax.numpy as jnp
from jax import lax
from jax.experimental import pallas as pl
from jax.experimental.pallas import tpu as pltpu
from jax.sharding import PartitionSpec as P


HEADS = 8
HEAD_DIM = 128
SPAN = 128
HALF = HEADS // 2
PIECE = HEAD_DIM + 8
OFFSETS = ((0, 1, 2, 3), (0, 2, 3, 1))

VM = pl.BlockSpec(memory_space=pltpu.VMEM)
HBM = pl.BlockSpec(memory_space=pltpu.HBM)


def place():
    me = lax.axis_index("block")
    return me & 1, (me >> 1) & 3, me >> 3


def offset_of(core, slot):
    return jnp.where(core == 0, OFFSETS[0][slot], OFFSETS[1][slot])


def head_columns(mine, slot):
    core, local, _ = place()
    core = core if mine else 1 - core
    head = core * HALF + (offset_of(core, slot) ^ local)
    return pl.ds(pl.multiple_of(head * HEAD_DIM, HEAD_DIM), HEAD_DIM)


def features(x):
    x = x.astype(jnp.float32)
    return jnp.where(x > 0, x + 1.0, jnp.exp(x)).astype(jnp.bfloat16)


def key_states(count, k_ref, v_ref, fk_ref, pf_ref, nf_ref, t_ref):
    acc = jnp.zeros((HEAD_DIM, HEAD_DIM), jnp.float32)
    norm = jnp.zeros((1, HEAD_DIM), jnp.float32)
    for c in range(count):
        rows = pl.ds(c * SPAN, SPAN)
        fk = features(k_ref[rows, :])
        fk_ref[rows, :] = fk
        pf_ref[rows, :] = acc
        nf_ref[pl.ds(c, 1), :] = norm
        acc = acc + lax.dot_general(
            fk, v_ref[rows, :], (((0,), (0,)), ((), ())), preferred_element_type=jnp.float32
        )
        norm = norm + jnp.sum(fk.astype(jnp.float32), axis=0, keepdims=True)
    t_ref[pl.ds(0, HEAD_DIM), :] = acc
    t_ref[pl.ds(HEAD_DIM, 8), :] = jnp.broadcast_to(norm, (8, HEAD_DIM))


def pre_a(count, early, k_hbm, v_hbm, k_ref, v_ref, *rest):
    *out_refs, sems = rest
    copies = []
    for j in range(HEADS):
        cols = head_columns(j >= HALF, j % HALF)
        ck = pltpu.make_async_copy(k_hbm.at[:, cols], k_ref.at[j], sems.at[0, j])
        cv = pltpu.make_async_copy(v_hbm.at[:, cols], v_ref.at[j], sems.at[1, j])
        ck.start()
        cv.start()
        copies.append((ck, cv))
    for j in range(HEADS):
        copies[j][0].wait()
        copies[j][1].wait()
        if j < HALF + early:
            at, outs = (j, out_refs[:4]) if j < HALF else (j - HALF, out_refs[4:])
            key_states(count, k_ref.at[j], v_ref.at[j], *(o.at[at] for o in outs))


def pre_b(count, early, k_ref, v_ref, *out_refs):
    for s in range(HALF - early):
        j = HALF + early + s
        key_states(count, k_ref.at[j], v_ref.at[j], *(o.at[s] for o in out_refs))


def pick(refs, slot):
    for ref in refs:
        if slot < ref.shape[0]:
            return ref.at[slot]
        slot -= ref.shape[0]


def mid(count, mine, parts, q_ref, *refs):
    fk_refs, nf_refs = refs[:parts], refs[parts : 2 * parts]
    fqs_ref, den_ref, done_ref = refs[2 * parts :]
    done_ref[...] = jnp.zeros_like(done_ref)
    causal = lax.broadcasted_iota(jnp.int32, (SPAN, SPAN), 0) >= lax.broadcasted_iota(
        jnp.int32, (SPAN, SPAN), 1
    )
    for s in range(HALF):
        cols = head_columns(mine, s)
        fk_ref, nf_ref = pick(fk_refs, s), pick(nf_refs, s)
        for c in range(count):
            rows = pl.ds(c * SPAN, SPAN)
            fq = features(q_ref[rows, cols])
            scores = lax.dot_general(
                fq, fk_ref[rows, :], (((1,), (1,)), ((), ())), preferred_element_type=jnp.float32
            )
            scores = jnp.where(causal, scores, 0.0)
            den = jnp.sum(
                scores + fq.astype(jnp.float32) * nf_ref[pl.ds(c, 1), :], axis=-1, keepdims=True
            )
            fqs_ref[s, rows, pl.ds(0, HEAD_DIM)] = fq
            fqs_ref[s, rows, pl.ds(HEAD_DIM, SPAN)] = scores.astype(jnp.bfloat16)
            den_ref[s, rows, :] = jnp.broadcast_to(den, (SPAN, HEAD_DIM))


def post(count, mine, parts, fqs_ref, den_ref, v_ref, b_ref, *rest):
    pf_refs = rest[:parts]
    o_hbm, o_ref, sems = rest[-3:]
    core, local, _ = place()
    core = core if mine else 1 - core
    width = HALF * HEAD_DIM
    half_cols = pl.ds(pl.multiple_of(core * width, width), width)
    first = HALF if mine else 0
    copies = []
    for c in range(count):
        rows = pl.ds(c * SPAN, SPAN)
        for s in range(HALF):
            fqs = fqs_ref[s, rows, :]
            prior = (pick(pf_refs, s)[rows, :] + b_ref[s, pl.ds(0, HEAD_DIM), :]).astype(
                jnp.bfloat16
            )
            num = jnp.dot(
                fqs,
                jnp.concatenate([prior, v_ref[first + s, rows, :]], axis=0),
                preferred_element_type=jnp.float32,
            )
            fq = fqs[:, :HEAD_DIM].astype(jnp.float32)
            den = den_ref[s, rows, :] + jnp.sum(
                fq * b_ref[s, pl.ds(HEAD_DIM, 1), :], axis=-1, keepdims=True
            )
            at = (offset_of(core, s) ^ local) * HEAD_DIM
            o_ref[rows, pl.ds(pl.multiple_of(at, HEAD_DIM), HEAD_DIM)] = (num / den).astype(
                jnp.bfloat16
            )
        copy = pltpu.make_async_copy(o_ref.at[rows, :], o_hbm.at[rows, half_cols], sems.at[c])
        copy.start()
        copies.append(copy)
    for copy in copies:
        copy.wait()


def add_totals(keep_parts, got_ref, *refs):
    keep_refs, piece_refs = refs[:keep_parts], refs[keep_parts:]
    for s in range(HALF):
        piece_refs[s][...] = pick(keep_refs, s)[...] + got_ref[s]


def inside_group(p0, p1, p2, p3, tied, e0, e1, e2, e3, total_ref):
    core, local, _ = place()
    pieces = [p[...] for p in (p0, p1, p2, p3)]
    chips = [local ^ offset_of(core, s) for s in range(4)]
    for s, e in enumerate((e0, e1, e2, e3)):
        acc = jnp.zeros((PIECE, HEAD_DIM), jnp.float32)
        for o in range(4):
            if o != s:
                acc = acc + jnp.where(chips[o] < chips[s], pieces[o], 0.0)
        e[...] = acc
    total_ref[...] = (pieces[0] + pieces[1]) + (pieces[2] + pieces[3])


def across_groups(bit, e0, e1, e2, e3, total_ref, got_ref, tied, f0, f1, f2, f3, *sum_ref):
    _, _, group = place()
    got = got_ref[...]
    earlier = jnp.where((group & bit) != 0, got, 0.0)
    for e, f in zip((e0, e1, e2, e3), (f0, f1, f2, f3)):
        f[...] = e[...] + earlier
    for ref in sum_ref:
        ref[...] = total_ref[...] + got


def both_cores(keep_parts, b0, b1, b2, b3, got_ref, *refs):
    keep_refs = refs[:keep_parts]
    mine_ref, send_ref = refs[keep_parts:]
    core, _, _ = place()
    for s, b in enumerate((b0, b1, b2, b3)):
        before = b[...]
        mine_ref[s] = before + jnp.where(core == 1, got_ref[s], 0.0)
        send_ref[s] = before + jnp.where(core == 0, pick(keep_refs, s)[...], 0.0)


def per_device(queries, keys, values):
    rows = queries.shape[0]
    count = rows // SPAN
    devices_n = lax.axis_size("block")
    groups_n = devices_n // 8
    assert groups_n * 8 == devices_n and groups_n & (groups_n - 1) == 0

    f32, bf16 = jnp.float32, jnp.bfloat16
    sds = jax.ShapeDtypeStruct

    def state_shapes(slots):
        return (
            sds((slots, rows, HEAD_DIM), bf16),
            sds((slots, rows, HEAD_DIM), f32),
            sds((slots, (count + 7) // 8 * 8, HEAD_DIM), f32),
            sds((slots, PIECE, HEAD_DIM), f32),
        )

    half_flops = HALF * count * 2 * SPAN * HEAD_DIM * HEAD_DIM

    def call(kernel, ins, outs, in_specs=None, out_specs=None, grant=8, flops=half_flops, nbytes=8 << 20, **more):
        return pl.pallas_call(
            kernel,
            out_shape=outs,
            in_specs=in_specs or [VM] * len(ins),
            out_specs=out_specs or (VM,) * len(outs),
            compiler_params=pltpu.CompilerParams(vmem_limit_bytes=grant << 20),
            cost_estimate=pl.CostEstimate(flops=flops, bytes_accessed=nbytes, transcendentals=0),
            **more,
        )(*ins)

    def small(kernel, ins, outs):
        return call(kernel, ins, outs, flops=1 << 20, nbytes=1 << 19)

    def swap(x, distance):
        return lax.ppermute(x, "block", [(i, i ^ distance) for i in range(devices_n)])

    def swap_slot(x, slot):
        return lax.ppermute(
            x, "block", [(i, i ^ (2 * OFFSETS[i & 1][slot])) for i in range(devices_n)]
        )

    early = 1
    k_vm, v_vm, *states = call(
        functools.partial(pre_a, count, early),
        (keys, values),
        (sds((HEADS, rows, HEAD_DIM), bf16),) * 2
        + state_shapes(HALF)
        + (state_shapes(early) if early else ()),
        in_specs=[HBM, HBM],
        grant=40,
        scratch_shapes=[pltpu.SemaphoreType.DMA((2, HEADS))],
    )
    fk_a, pf_a, nf_a, t_send = states[:4]
    t_got = swap(t_send, 1)
    late = call(functools.partial(pre_b, count, early), (k_vm, v_vm), state_shapes(HALF - early))
    fk_b, pf_b, nf_b, t_keep = ([x, y] for x, y in zip(states[4:], late)) if early else ([x] for x in late)

    def mid_call(mine, fk, nf):
        return call(
            functools.partial(mid, count, mine, len(fk)),
            (queries, *fk, *nf),
            (
                sds((HALF, rows, 2 * HEAD_DIM), bf16),
                sds((HALF, rows, HEAD_DIM), f32),
                sds((8, HEAD_DIM), f32),
            ),
        )

    piece = sds((PIECE, HEAD_DIM), f32)

    pieces = small(functools.partial(add_totals, len(t_keep)), (t_got, *t_keep), (piece,) * 4)
    landed = {}
    for s in (2, 3, 1):
        landed[s] = swap_slot(pieces[s], s)
    fqs_b, den_b, done_b = mid_call(True, fk_b, nf_b)
    *finals, total = small(
        inside_group, (pieces[0], landed[1], landed[2], landed[3], done_b), (piece,) * 5
    )
    fqs_a, den_a, done_a = mid_call(False, [fk_a], [nf_a])
    bit = 1
    while bit < groups_n:
        got = swap(total, 8 * bit)
        sums = 1 if 2 * bit < groups_n else 0
        finals = small(
            functools.partial(across_groups, bit),
            (*finals[:4], total, got, done_a),
            (piece,) * (4 + sums),
        )
        total = finals[-1]
        bit *= 2
    back = {0: finals[0]}
    for s in (2, 3, 1):
        back[s] = swap_slot(finals[s], s)
    four = sds((HALF, PIECE, HEAD_DIM), f32)
    before_b, send_a = small(
        functools.partial(both_cores, len(t_keep)),
        (back[0], back[1], back[2], back[3], t_got, *t_keep),
        (four, four),
    )
    before_a = swap(send_a, 1)

    out = None
    for mine, fqs, den, pf, b in (
        (True, fqs_b, den_b, pf_b, before_b),
        (False, fqs_a, den_a, [pf_a], before_a),
    ):
        ins = (fqs, den, v_vm, b, *pf)
        extra = () if out is None else (out,)
        out = call(
            functools.partial(post, count, mine, len(pf)),
            (*ins, *extra),
            sds((rows, HEADS * HEAD_DIM), bf16),
            in_specs=[VM] * len(ins) + [HBM] * len(extra),
            out_specs=HBM,
            scratch_shapes=[
                pltpu.VMEM((rows, HALF * HEAD_DIM), bf16),
                pltpu.SemaphoreType.DMA((count,)),
            ],
            input_output_aliases={len(ins): 0} if extra else {},
        )
    return out


def solution(mesh):
    placed = P(("groups", "block"), None)

    return jax.shard_map(
        per_device,
        mesh=mesh,
        in_specs=(placed, placed, placed),
        out_specs=placed,
        check_vma=False,
    )
```

time: 35.9 us -> 32.4 us (0.903)
  Pallas kernels: 16.1 us -> 12.3 us
  starting transfers between devices: 9.24 us -> 11.3 us
  waiting for transfers between devices: 10.3 us -> 8.57 us
    pallas_call x13 -> x10, Pallas kernels: 16.1 us -> 12.3 us  [call(): pl.pallas_call(kernel, out_shape=outs, in_specs=in_specs or [VM] * len(in...]
    ppermute x6, starting transfers between devices: 5.88 us -> 8.05 us  [swap_slot(): lax.ppermute(x, 'block', [(i, i ^ 2 * OFFSETS[i & 1][slot]) for i in rang...]
    ppermute x6, waiting for transfers between devices: 8.55 us -> 6.68 us  [swap_slot(): lax.ppermute(x, 'block', [(i, i ^ 2 * OFFSETS[i & 1][slot]) for i in rang...]
    ppermute x4 -> x3, waiting for transfers between devices: 1.73 us -> 1.89 us  [swap(): lax.ppermute(x, 'block', [(i, i ^ distance) for i in range(devices_n)])]
    ppermute x4 -> x3, starting transfers between devices: 3.36 us -> 3.28 us  [swap(): lax.ppermute(x, 'block', [(i, i ^ distance) for i in range(devices_n)])]
  transfers between devices with their start and end apart: 10 -> 9, of which waited for: 5 -> 7; matrix products, arithmetic and copies ran while one was open for 0% -> 0% of each run, Pallas kernels for 28% -> 20%
where the time goes in v1:
time: 32.4 us; the launch traced here: 32.3 us
  Pallas kernels  12.3 us (38%)
  starting transfers between devices  11.3 us (35%)
  waiting for transfers between devices  8.57 us (26%)
    pallas_call x10, Pallas kernels, call(): pl.pallas_call(kernel, out_shape=outs, in_specs=in_specs or [VM] * len(in...  12.3 us
    ppermute x6, starting transfers between devices, swap_slot(): lax.ppermute(x, 'block', [(i, i ^ 2 * OFFSETS[i & 1][slot]) for i in rang...  8.05 us
    ppermute x6, waiting for transfers between devices, swap_slot(): lax.ppermute(x, 'block', [(i, i ^ 2 * OFFSETS[i & 1][slot]) for i in rang...  6.68 us
    ppermute x3, starting transfers between devices, swap(): lax.ppermute(x, 'block', [(i, i ^ distance) for i in range(devices_n)])  3.28 us
    ppermute x3, waiting for transfers between devices, swap(): lax.ppermute(x, 'block', [(i, i ^ distance) for i in range(devices_n)])  1.89 us
  transfers between devices with their start and end apart: 9, of which 7 were waited for; matrix products, arithmetic and copies ran while one was open for 0% of the time, Pallas kernels for 20%

profile of v1, /device:TPU:0, one launch (start us, length us, event | category | flops | bytes accessed | tf_op | source)
XLA Modules:
  0.0 32.3 jit_solution(11887505710036582886)
XLA Ops:
  0.0 3.5 %shard_map.37 = (bf16[8,1536,128]{2,1,0:T(8,128)(2,1)S(1)}, bf16[8,1536,128]{2,1,0:T(8,128)(2,1)S(1)}, bf16[4,1536,128]{2,1,0:T(8,128)(2,1)S(1)}, f32[4,1536,128...) custom-call(bf16[1536,1024]{1,0:T(8,128)(2,1)} %k_hbm.1, ...), custom_call_target="tpu_custom_call" | custom-call | flops 201326592 | bytes 8388608 | tf_op jit(solution)/shard_map/pallas_call | solution.py:212
  3.5 0.6 %collective-permute-start = (f32[4,136,128]{2,1,0:T(8,128)S(1)}, f32[4,136,128]{2,1,0:T(8,128)S(1)}, u32[]{:S(2)}, u32[]{:S(2)}) collective-permute-start(f32[4,136,128]{2,1,0:T(8,128)S(1)} %get-tuple-element.45), channel_id=1, source_target_pairs={{0,1},{1,0},{2,3},{3,2},{4,5},{5,4},{6,7},{7,6},{8,9},{9,8},{10,11... | collective-permute-start | bytes 835592 | tf_op jit(solution)/shard_map/ppermute | solution.py:226
  4.1 0.0 copy-start
  4.1 1.0 %shard_map.39 = (bf16[3,1536,128]{2,1,0:T(8,128)(2,1)S(1)}, f32[3,1536,128]{2,1,0:T(8,128)S(1)}, f32[3,16,128]{2,1,0:T(8,128)S(1)}, f32[3,136,128]{2,1,0:T(8,128)S(1)}) custom-call(bf16[8,1536,128]{2,1,0:T(8,128)(2,1)S(1)} %get-tuple-element.47.k_ref, bf16[8,1536,128]{2,1,0:T(8,128)(2,1)S(1)} %get-tuple-element.44.v_ref), custom_call_target="tpu_custom_call" | custom-call | flops 201326592 | bytes 8388608 | tf_op jit(solution)/shard_map/pallas_call | solution.py:212
  5.1 0.1 collective-permute-done.got_ref
  5.3 2.9 %collective-permute-start.1 = (f32[136,128]{1,0:T(8,128)S(1)}, f32[136,128]{1,0:T(8,128)S(1)}, u32[]{:S(2)}, u32[]{:S(2)}) collective-permute-start(f32[136,128]{1,0:T(8,128)S(1)} %get-tuple-element.50), channel_id=1, source_target_pairs={{0,2},{1,5},{2,0},{3,7},{4,6},{5,1},{6,4},{7,3},{8,10},{9,13},{10,... | collective-permute-start | bytes 208904 | tf_op jit(solution)/shard_map/ppermute | solution.py:229
  8.2 1.6 %collective-permute-start.2 = (f32[136,128]{1,0:T(8,128)S(1)}, f32[136,128]{1,0:T(8,128)S(1)}, u32[]{:S(2)}, u32[]{:S(2)}) collective-permute-start(f32[136,128]{1,0:T(8,128)S(1)} %get-tuple-element.51), channel_id=1, source_target_pairs={{0,4},{1,7},{2,6},{3,5},{4,0},{5,3},{6,2},{7,1},{8,12},{9,15},{10,... | collective-permute-start | bytes 208904 | tf_op jit(solution)/shard_map/ppermute | solution.py:229
  9.8 0.0 collective-permute-start.3
  9.8 0.0 copy-done
  9.8 1.5 %shard_map.41 = (bf16[4,1536,256]{2,1,0:T(8,128)(2,1)S(1)}, f32[4,1536,128]{2,1,0:T(8,128)S(1)}, f32[8,128]{1,0:T(8,128)S(1)}) custom-call(bf16[1536,1024]{1,0:T(8,128)(2,1)S(1)} %copy-done, bf16[1,1536,128]{2,1,0:T(8,128)(2,1)S(1)} %get-tuple-element.53.refs_0_, bf16[3,1536,128]{2,1,0:T(8,128)(2,1)S(1)} %get-tuple-element.54.refs_1_, ...), custom_call_target="tpu_custom_call" | custom-call | flops 201326592 | bytes 8388608 | tf_op jit(solution)/shard_map/pallas_call | solution.py:212
  11.3 0.0 collective-permute-done.1.p1
  11.3 1.8 %collective-permute-done.2.p2 = f32[136,128]{1,0:T(8,128)S(1)} collective-permute-done((f32[136,128]{1,0:T(8,128)S(1)}, f32[136,128]{1,0:T(8,128)S(1)}, u32[]{:S(2)}, u32[]{:S(2)}) %collective-permute-start.2) | collective-permute-done | bytes 69664 | tf_op jit(solution)/shard_map/ppermute | solution.py:229
  13.2 1.8 %collective-permute-done.3.p3 = f32[136,128]{1,0:T(8,128)S(1)} collective-permute-done((f32[136,128]{1,0:T(8,128)S(1)}, f32[136,128]{1,0:T(8,128)S(1)}, u32[]{:S(2)}, u32[]{:S(2)}) %collective-permute-start.3) | collective-permute-done | bytes 69664 | tf_op jit(solution)/shard_map/ppermute | solution.py:229
  15.0 0.1 shard_map.42
  15.1 2.7 %collective-permute-start.4 = (f32[136,128]{1,0:T(8,128)S(1)}, f32[136,128]{1,0:T(8,128)S(1)}, u32[]{:S(2)}, u32[]{:S(2)}) collective-permute-start(f32[136,128]{1,0:T(8,128)S(1)} %get-tuple-element.62.total_ref), channel_id=1, source_target_pairs={{0,8},{1,9},{2,10},{3,11},{4,12},{5,13},{6,14},{7,15},{8,0},{9,1},... | collective-permute-start | bytes 208904 | tf_op jit(solution)/shard_map/ppermute | solution.py:226
  17.7 1.5 %shard_map.38 = (bf16[4,1536,256]{2,1,0:T(8,128)(2,1)S(1)}, f32[4,1536,128]{2,1,0:T(8,128)S(1)}, f32[8,128]{1,0:T(8,128)S(1)}) custom-call(bf16[1536,1024]{1,0:T(8,128)(2,1)S(1)} %copy-done, bf16[4,1536,128]{2,1,0:T(8,128)(2,1)S(1)} %get-tuple-element.40.refs_0_, f32[4,16,128]{2,1,0:T(8,128)S(1)} %get-tuple-element.41.refs_1_), custom_call_target="tpu_custom_call" | custom-call | flops 201326592 | bytes 8388608 | tf_op jit(solution)/shard_map/pallas_call | solution.py:212
  19.2 1.7 %collective-permute-done.4.got_ref = f32[136,128]{1,0:T(8,128)S(1)} collective-permute-done((f32[136,128]{1,0:T(8,128)S(1)}, f32[136,128]{1,0:T(8,128)S(1)}, u32[]{:S(2)}, u32[]{:S(2)}) %collective-permute-start.4) | collective-permute-done | bytes 69664 | tf_op jit(solution)/shard_map/ppermute | solution.py:226
  21.0 0.8 %collective-permute-start.5 = (f32[136,128]{1,0:T(8,128)S(1)}, f32[136,128]{1,0:T(8,128)S(1)}, u32[]{:S(2)}, u32[]{:S(2)}) collective-permute-start(f32[136,128]{1,0:T(8,128)S(1)} %get-tuple-element.65), channel_id=1, source_target_pairs={{0,2},{1,5},{2,0},{3,7},{4,6},{5,1},{6,4},{7,3},{8,10},{9,13},{10,... | collective-permute-start | bytes 208904 | tf_op jit(solution)/shard_map/ppermute | solution.py:229
  21.8 0.1 collective-permute-start.6
  21.9 2.7 %collective-permute-start.7 = (f32[136,128]{1,0:T(8,128)S(1)}, f32[136,128]{1,0:T(8,128)S(1)}, u32[]{:S(2)}, u32[]{:S(2)}) collective-permute-start(f32[136,128]{1,0:T(8,128)S(1)} %get-tuple-element.67), channel_id=1, source_target_pairs={{0,6},{1,3},{2,4},{3,1},{4,2},{5,7},{6,0},{7,5},{8,14},{9,11},{10,... | collective-permute-start | bytes 208904 | tf_op jit(solution)/shard_map/ppermute | solution.py:229
  24.6 0.8 %collective-permute-done.5.b1 = f32[136,128]{1,0:T(8,128)S(1)} collective-permute-done((f32[136,128]{1,0:T(8,128)S(1)}, f32[136,128]{1,0:T(8,128)S(1)}, u32[]{:S(2)}, u32[]{:S(2)}) %collective-permute-start.5) | collective-permute-done | bytes 69664 | tf_op jit(solution)/shard_map/ppermute | solution.py:229
  25.4 0.7 %collective-permute-done.6.b2 = f32[136,128]{1,0:T(8,128)S(1)} collective-permute-done((f32[136,128]{1,0:T(8,128)S(1)}, f32[136,128]{1,0:T(8,128)S(1)}, u32[]{:S(2)}, u32[]{:S(2)}) %collective-permute-start.6) | collective-permute-done | bytes 69664 | tf_op jit(solution)/shard_map/ppermute | solution.py:229
  26.1 1.5 %collective-permute-done.7.b3 = f32[136,128]{1,0:T(8,128)S(1)} collective-permute-done((f32[136,128]{1,0:T(8,128)S(1)}, f32[136,128]{1,0:T(8,128)S(1)}, u32[]{:S(2)}, u32[]{:S(2)}) %collective-permute-start.7) | collective-permute-done | bytes 69664 | tf_op jit(solution)/shard_map/ppermute | solution.py:229
  27.6 0.1 shard_map.44
  27.7 0.1 collective-permute-start.8
  27.8 2.3 %shard_map.45.rest_1_ = bf16[1536,1024]{1,0:T(8,128)(2,1)} custom-call(bf16[4,1536,256]{2,1,0:T(8,128)(2,1)S(1)} %get-tuple-element.70.fqs_ref, f32[4,1536,128]{2,1,0:T(8,128)S(1)} %get-tuple-element.71.den_ref, bf16[8,1536,128]{2,1,0:T(8,128)(2,1)S(1)} %get-tuple-element.44.v_ref, f32[4,136,128]{2,1,0:T(8,128)S(1)} %get-tuple-element.72.b_ref, ...), custom_call_target="tpu_custom_call" | custom-call | flops 201326592 | bytes 8388608 | tf_op jit(solution)/shard_map/pallas_call | solution.py:212
  30.1 0.0 collective-permute-done.8.b_ref
  30.1 2.2 %shard_map.46 = bf16[1536,1024]{1,0:T(8,128)(2,1)} custom-call(bf16[4,1536,256]{2,1,0:T(8,128)(2,1)S(1)} %get-tuple-element.42.fqs_ref, f32[4,1536,128]{2,1,0:T(8,128)S(1)} %get-tuple-element.43.den_ref, bf16[8,1536,128]{2,1,0:T(8,128)(2,1)S(1)} %get-tuple-element.44.v_ref, ...), custom_call_target="tpu_custom_call", output_to_operand_aliasing={{}: (5, {})} | custom-call | flops 201326592 | bytes 8388608 | tf_op jit(solution)/shard_map/pallas_call | solution.py:212
  (2 shorter events, 0.1 us)
Async XLA Ops:
  3.5 1.7 %collective-permute-start = (f32[4,136,128]{2,1,0:T(8,128)S(1)}, f32[4,136,128]{2,1,0:T(8,128)S(1)}, u32[]{:S(2)}, u32[]{:S(2)}) collective-permute-start(f32[4,136,128]{2,1,0:T(8,128)S(1)} %get-tuple-element.45), channel_id=1, source_target_pairs={{0,1},{1,0},{2,3},{3,2},{4,5},{5,4},{6,7},{7,6},{8,9},{9,8},{10,11... | collective-permute-start | bytes 835592 | tf_op jit(solution)/shard_map/ppermute | solution.py:226
  4.1 5.7 %copy-start = (bf16[1536,1024]{1,0:T(8,128)(2,1)S(1)}, bf16[1536,1024]{1,0:T(8,128)(2,1)}, u32[]{:S(2)}) copy-start(bf16[1536,1024]{1,0:T(8,128)(2,1)} %q_ref.3) | copy-start | bytes 9437188
  5.3 6.0 %collective-permute-start.1 = (f32[136,128]{1,0:T(8,128)S(1)}, f32[136,128]{1,0:T(8,128)S(1)}, u32[]{:S(2)}, u32[]{:S(2)}) collective-permute-start(f32[136,128]{1,0:T(8,128)S(1)} %get-tuple-element.50), channel_id=1, source_target_pairs={{0,2},{1,5},{2,0},{3,7},{4,6},{5,1},{6,4},{7,3},{8,10},{9,13},{10,... | collective-permute-start | bytes 208904 | tf_op jit(solution)/shard_map/ppermute | solution.py:229
  8.2 5.0 %collective-permute-start.2 = (f32[136,128]{1,0:T(8,128)S(1)}, f32[136,128]{1,0:T(8,128)S(1)}, u32[]{:S(2)}, u32[]{:S(2)}) collective-permute-start(f32[136,128]{1,0:T(8,128)S(1)} %get-tuple-element.51), channel_id=1, source_target_pairs={{0,4},{1,7},{2,6},{3,5},{4,0},{5,3},{6,2},{7,1},{8,12},{9,15},{10,... | collective-permute-start | bytes 208904 | tf_op jit(solution)/shard_map/ppermute | solution.py:229
  9.8 5.2 %collective-permute-start.3 = (f32[136,128]{1,0:T(8,128)S(1)}, f32[136,128]{1,0:T(8,128)S(1)}, u32[]{:S(2)}, u32[]{:S(2)}) collective-permute-start(f32[136,128]{1,0:T(8,128)S(1)} %get-tuple-element.52), channel_id=1, source_target_pairs={{0,6},{1,3},{2,4},{3,1},{4,2},{5,7},{6,0},{7,5},{8,14},{9,11},{10,... | collective-permute-start | bytes 208904 | tf_op jit(solution)/shard_map/ppermute | solution.py:229
  15.1 5.9 %collective-permute-start.4 = (f32[136,128]{1,0:T(8,128)S(1)}, f32[136,128]{1,0:T(8,128)S(1)}, u32[]{:S(2)}, u32[]{:S(2)}) collective-permute-start(f32[136,128]{1,0:T(8,128)S(1)} %get-tuple-element.62.total_ref), channel_id=1, source_target_pairs={{0,8},{1,9},{2,10},{3,11},{4,12},{5,13},{6,14},{7,15},{8,0},{9,1},... | collective-permute-start | bytes 208904 | tf_op jit(solution)/shard_map/ppermute | solution.py:226
  21.0 4.4 %collective-permute-start.5 = (f32[136,128]{1,0:T(8,128)S(1)}, f32[136,128]{1,0:T(8,128)S(1)}, u32[]{:S(2)}, u32[]{:S(2)}) collective-permute-start(f32[136,128]{1,0:T(8,128)S(1)} %get-tuple-element.65), channel_id=1, source_target_pairs={{0,2},{1,5},{2,0},{3,7},{4,6},{5,1},{6,4},{7,3},{8,10},{9,13},{10,... | collective-permute-start | bytes 208904 | tf_op jit(solution)/shard_map/ppermute | solution.py:229
  21.8 4.3 %collective-permute-start.6 = (f32[136,128]{1,0:T(8,128)S(1)}, f32[136,128]{1,0:T(8,128)S(1)}, u32[]{:S(2)}, u32[]{:S(2)}) collective-permute-start(f32[136,128]{1,0:T(8,128)S(1)} %get-tuple-element.66), channel_id=1, source_target_pairs={{0,4},{1,7},{2,6},{3,5},{4,0},{5,3},{6,2},{7,1},{8,12},{9,15},{10,... | collective-permute-start | bytes 208904 | tf_op jit(solution)/shard_map/ppermute | solution.py:229
  21.9 5.7 %collective-permute-start.7 = (f32[136,128]{1,0:T(8,128)S(1)}, f32[136,128]{1,0:T(8,128)S(1)}, u32[]{:S(2)}, u32[]{:S(2)}) collective-permute-start(f32[136,128]{1,0:T(8,128)S(1)} %get-tuple-element.67), channel_id=1, source_target_pairs={{0,6},{1,3},{2,4},{3,1},{4,2},{5,7},{6,0},{7,5},{8,14},{9,11},{10,... | collective-permute-start | bytes 208904 | tf_op jit(solution)/shard_map/ppermute | solution.py:229
  27.7 2.4 %collective-permute-start.8 = (f32[4,136,128]{2,1,0:T(8,128)S(1)}, f32[4,136,128]{2,1,0:T(8,128)S(1)}, u32[]{:S(2)}, u32[]{:S(2)}) collective-permute-start(f32[4,136,128]{2,1,0:T(8,128)S(1)} %get-tuple-element.68), channel_id=1, source_target_pairs={{0,1},{1,0},{2,3},{3,2},{4,5},{5,4},{6,7},{7,6},{8,9},{9,8},{10,11... | collective-permute-start | bytes 835592 | tf_op jit(solution)/shard_map/ppermute | solution.py:226

commit v2 on v0

v2 whole, which is shorter than its diff:
```python
import functools

import jax
import jax.numpy as jnp
from jax import lax
from jax.experimental import pallas as pl
from jax.experimental.pallas import tpu as pltpu
from jax.sharding import PartitionSpec as P


HEADS = 8
HEAD_DIM = 128
SPAN = 128
HALF = HEADS // 2
PIECE = HEAD_DIM + 8
READS = 1
SLOT_ORDER = (3, 2, 1)

VM = pl.BlockSpec(memory_space=pltpu.VMEM)
HBM = pl.BlockSpec(memory_space=pltpu.HBM)


def place():
    me = lax.axis_index("block")
    return me & 1, (me >> 1) & 3, me >> 3


def head_columns(mine, slot):
    core, local, _ = place()
    core = core if mine else 1 - core
    head = core * HALF + (slot ^ local)
    return pl.ds(pl.multiple_of(head * HEAD_DIM, HEAD_DIM), HEAD_DIM)


def features(x):
    x = x.astype(jnp.float32)
    return jnp.where(x > 0, x + 1.0, jnp.exp(x)).astype(jnp.bfloat16)


def key_states(count, k_ref, v_ref, fk_ref, pf_ref, nf_ref, t_ref):
    acc = jnp.zeros((HEAD_DIM, HEAD_DIM), jnp.float32)
    norm = jnp.zeros((1, HEAD_DIM), jnp.float32)
    for c in range(count):
        rows = pl.ds(c * SPAN, SPAN)
        fk = features(k_ref[rows, :])
        fk_ref[rows, :] = fk
        pf_ref[rows, :] = acc
        nf_ref[pl.ds(c, 1), :] = norm
        acc = acc + lax.dot_general(
            fk, v_ref[rows, :], (((0,), (0,)), ((), ())), preferred_element_type=jnp.float32
        )
        norm = norm + jnp.sum(fk.astype(jnp.float32), axis=0, keepdims=True)
    t_ref[pl.ds(0, HEAD_DIM), :] = acc
    t_ref[pl.ds(HEAD_DIM, 8), :] = jnp.broadcast_to(norm, (8, HEAD_DIM))


def pre_a(count, k_hbm, v_hbm, k_ref, v_ref, *rest):
    *out_refs, sems = rest

    part = count * SPAN // READS

    def copies(j, i):
        cols = head_columns(j >= HALF, j % HALF)
        rows = pl.ds(i * part, part)
        return (
            pltpu.make_async_copy(k_hbm.at[rows, cols], k_ref.at[j, rows], sems.at[0, j, i]),
            pltpu.make_async_copy(v_hbm.at[rows, cols], v_ref.at[j, rows], sems.at[1, j, i]),
        )

    def each(j, act):
        for i in range(READS):
            for copy in copies(j, i):
                act(copy)

    for j in range(HEADS):
        each(j, lambda copy: copy.start())
    for j in range(HEADS):
        each(j, lambda copy: copy.wait())
        if j < HALF:
            key_states(count, k_ref.at[j], v_ref.at[j], *(o.at[j] for o in out_refs))


def pre_b(count, k_ref, v_ref, *out_refs):
    for s in range(HALF):
        key_states(count, k_ref.at[HALF + s], v_ref.at[HALF + s], *(o.at[s] for o in out_refs))


def queries_of(count, mine, q_ref, fk_ref, nf_ref, fqs_ref, den_ref):
    causal = lax.broadcasted_iota(jnp.int32, (SPAN, SPAN), 0) >= lax.broadcasted_iota(
        jnp.int32, (SPAN, SPAN), 1
    )
    for s in range(HALF):
        cols = head_columns(mine, s)
        for c in range(count):
            rows = pl.ds(c * SPAN, SPAN)
            fq = features(q_ref[rows, cols])
            scores = lax.dot_general(
                fq, fk_ref[s, rows, :], (((1,), (1,)), ((), ())), preferred_element_type=jnp.float32
            )
            scores = jnp.where(causal, scores, 0.0)
            den = jnp.sum(
                scores + fq.astype(jnp.float32) * nf_ref[s, pl.ds(c, 1), :], axis=-1, keepdims=True
            )
            fqs_ref[s, rows, pl.ds(0, HEAD_DIM)] = fq
            fqs_ref[s, rows, pl.ds(HEAD_DIM, SPAN)] = scores.astype(jnp.bfloat16)
            den_ref[s, rows, :] = jnp.broadcast_to(den, (SPAN, HEAD_DIM))


def mid_mine(count, q_ref, fk_ref, nf_ref, fqs_ref, den_ref, done_ref):
    done_ref[...] = jnp.zeros_like(done_ref)
    queries_of(count, True, q_ref, fk_ref, nf_ref, fqs_ref, den_ref)


def mid_other(count, q_ref, fk_ref, nf_ref, fqs_ref, den_ref, done_ref):
    done_ref[...] = jnp.zeros_like(done_ref)
    queries_of(count, False, q_ref, fk_ref, nf_ref, fqs_ref, den_ref)


def half_columns(mine):
    core, _, _ = place()
    width = HALF * HEAD_DIM
    return pl.ds(pl.multiple_of((core if mine else 1 - core) * width, width), width)


def attend(c, first, fqs_ref, den_ref, v_ref, b_ref, pf_ref, o_ref):
    _, local, _ = place()
    rows = pl.ds(c * SPAN, SPAN)
    for s in range(HALF):
        fqs = fqs_ref[s, rows, :]
        prior = (pf_ref[s, rows, :] + b_ref[s, pl.ds(0, HEAD_DIM), :]).astype(jnp.bfloat16)
        num = jnp.dot(
            fqs,
            jnp.concatenate([prior, v_ref[first + s, rows, :]], axis=0),
            preferred_element_type=jnp.float32,
        )
        fq = fqs[:, :HEAD_DIM].astype(jnp.float32)
        den = den_ref[s, rows, :] + jnp.sum(
            fq * b_ref[s, pl.ds(HEAD_DIM, 1), :], axis=-1, keepdims=True
        )
        at = (s ^ local) * HEAD_DIM
        o_ref[rows, pl.ds(pl.multiple_of(at, HEAD_DIM), HEAD_DIM)] = (num / den).astype(
            jnp.bfloat16
        )


def post_mine(count, fqs_ref, den_ref, v_ref, b_ref, pf_ref, o_ref):
    for c in range(count):
        attend(c, HALF, fqs_ref, den_ref, v_ref, b_ref, pf_ref, o_ref)


def post_other(count, fqs_ref, den_ref, v_ref, b_ref, pf_ref, mine_ref, o_hbm, o_ref, sems):
    def copy(c, mine):
        rows = pl.ds(c * SPAN, SPAN)
        return pltpu.make_async_copy(
            (mine_ref if mine else o_ref).at[rows, :],
            o_hbm.at[rows, half_columns(mine)],
            sems.at[int(mine), c],
        )

    for c in range(count):
        copy(c, True).start()
    for c in range(count):
        attend(c, 0, fqs_ref, den_ref, v_ref, b_ref, pf_ref, o_ref)
        copy(c, False).start()
    for c in range(count):
        copy(c, True).wait()
        copy(c, False).wait()


def add_totals(keep_ref, got_ref, *piece_refs):
    for s in range(HALF):
        piece_refs[s][...] = keep_ref[s] + got_ref[s]


def inside_group(p0, p1, p2, p3, tied, e0, e1, e2, e3, total_ref):
    _, local, _ = place()
    pieces = [p[...] for p in (p0, p1, p2, p3)]
    chips = [local ^ s for s in range(4)]
    for s, e in enumerate((e0, e1, e2, e3)):
        acc = jnp.zeros((PIECE, HEAD_DIM), jnp.float32)
        for o in range(4):
            if o != s:
                acc = acc + jnp.where(chips[o] < chips[s], pieces[o], 0.0)
        e[...] = acc
    total_ref[...] = (pieces[0] + pieces[1]) + (pieces[2] + pieces[3])


def across_groups(bit, e0, e1, e2, e3, total_ref, got_ref, tied, f0, f1, f2, f3, *sum_ref):
    _, _, group = place()
    got = got_ref[...]
    earlier = jnp.where((group & bit) != 0, got, 0.0)
    for e, f in zip((e0, e1, e2, e3), (f0, f1, f2, f3)):
        f[...] = e[...] + earlier
    for ref in sum_ref:
        ref[...] = total_ref[...] + got


def both_cores(b0, b1, b2, b3, keep_ref, got_ref, mine_ref, send_ref):
    core, _, _ = place()
    for s, b in enumerate((b0, b1, b2, b3)):
        before = b[...]
        mine_ref[s] = before + jnp.where(core == 1, got_ref[s], 0.0)
        send_ref[s] = before + jnp.where(core == 0, keep_ref[s], 0.0)


def per_device(queries, keys, values):
    rows = queries.shape[0]
    count = rows // SPAN
    devices_n = lax.axis_size("block")
    groups_n = devices_n // 8
    assert groups_n * 8 == devices_n and groups_n & (groups_n - 1) == 0

    f32, bf16 = jnp.float32, jnp.bfloat16
    sds = jax.ShapeDtypeStruct

    state_shapes = (
        sds((HALF, rows, HEAD_DIM), bf16),
        sds((HALF, rows, HEAD_DIM), f32),
        sds((HALF, (count + 7) // 8 * 8, HEAD_DIM), f32),
        sds((HALF, PIECE, HEAD_DIM), f32),
    )
    query_shapes = (
        sds((HALF, rows, 2 * HEAD_DIM), bf16),
        sds((HALF, rows, HEAD_DIM), f32),
    )
    token = sds((8, HEAD_DIM), f32)
    half_flops = HALF * count * 2 * SPAN * HEAD_DIM * HEAD_DIM

    def call(kernel, ins, outs, in_specs=None, out_specs=None, grant=8, flops=half_flops, nbytes=8 << 20, **more):
        return pl.pallas_call(
            kernel,
            out_shape=outs,
            in_specs=in_specs or [VM] * len(ins),
            out_specs=out_specs or (VM,) * len(outs),
            compiler_params=pltpu.CompilerParams(vmem_limit_bytes=grant << 20),
            cost_estimate=pl.CostEstimate(flops=flops, bytes_accessed=nbytes, transcendentals=0),
            **more,
        )(*ins)

    def small(kernel, ins, outs):
        return call(kernel, ins, outs, flops=1 << 20, nbytes=1 << 19)

    def swap(x, distance):
        return lax.ppermute(x, "block", [(i, i ^ distance) for i in range(devices_n)])

    def swap_slot(x, slot):
        return swap(x, 2 * slot)

    k_vm, v_vm, fk_a, pf_a, nf_a, t_send = call(
        functools.partial(pre_a, count),
        (keys, values),
        (sds((HEADS, rows, HEAD_DIM), bf16),) * 2 + state_shapes,
        in_specs=[HBM, HBM],
        grant=42,
        scratch_shapes=[pltpu.SemaphoreType.DMA((2, HEADS, READS))],
    )
    t_got = swap(t_send, 1)
    fk_b, pf_b, nf_b, t_keep = call(functools.partial(pre_b, count), (k_vm, v_vm), state_shapes)

    piece = sds((PIECE, HEAD_DIM), f32)

    pieces = small(add_totals, (t_keep, t_got), (piece,) * 4)
    landed = {}
    for s in SLOT_ORDER:
        landed[s] = swap_slot(pieces[s], s)
    fqs_b, den_b, done_b = call(
        functools.partial(mid_mine, count), (queries, fk_b, nf_b), (*query_shapes, token)
    )
    *finals, total = small(
        inside_group, (pieces[0], landed[1], landed[2], landed[3], done_b), (piece,) * 5
    )
    fqs_a, den_a, done_a = call(
        functools.partial(mid_other, count), (queries, fk_a, nf_a), (*query_shapes, token)
    )
    bit = 1
    while bit < groups_n:
        got = swap(total, 8 * bit)
        sums = 1 if 2 * bit < groups_n else 0
        finals = small(
            functools.partial(across_groups, bit),
            (*finals[:4], total, got, done_a),
            (piece,) * (4 + sums),
        )
        total = finals[-1]
        bit *= 2
    back = {0: finals[0]}
    for s in SLOT_ORDER:
        back[s] = swap_slot(finals[s], s)
    four = sds((HALF, PIECE, HEAD_DIM), f32)
    before_b, send_a = small(
        both_cores, (back[0], back[1], back[2], back[3], t_keep, t_got), (four, four)
    )
    before_a = swap(send_a, 1)

    (mine,) = call(
        functools.partial(post_mine, count),
        (fqs_b, den_b, v_vm, before_b, pf_b),
        (sds((rows, HALF * HEAD_DIM), bf16),),
    )
    return call(
        functools.partial(post_other, count),
        (fqs_a, den_a, v_vm, before_a, pf_a, mine),
        sds((rows, HEADS * HEAD_DIM), bf16),
        out_specs=HBM,
        scratch_shapes=[
            pltpu.VMEM((rows, HALF * HEAD_DIM), bf16),
            pltpu.SemaphoreType.DMA((2, count)),
        ],
    )


def solution(mesh):
    placed = P(("groups", "block"), None)

    return jax.shard_map(
        per_device,
        mesh=mesh,
        in_specs=(placed, placed, placed),
        out_specs=placed,
        check_vma=False,
    )
```

time: 35.9 us -> 31.3 us (0.87)
  Pallas kernels: 16.1 us -> 11 us
  starting transfers between devices: 9.24 us -> 11.2 us
  waiting for transfers between devices: 10.3 us -> 8.83 us
    ppermute x6 -> x0, waiting for transfers between devices: 8.55 us -> none  [swap_slot(): lax.ppermute(x, 'block', [(i, i ^ 2 * OFFSETS[i & 1][slot]) for i in rang...]
    ppermute x4 -> x9, starting transfers between devices: 3.36 us -> 11.2 us  [swap(): lax.ppermute(x, 'block', [(i, i ^ distance) for i in range(devices_n)])]
    ppermute x4 -> x9, waiting for transfers between devices: 1.73 us -> 8.83 us  [swap(): lax.ppermute(x, 'block', [(i, i ^ distance) for i in range(devices_n)])]
    ppermute x6 -> x0, starting transfers between devices: 5.88 us -> none  [swap_slot(): lax.ppermute(x, 'block', [(i, i ^ 2 * OFFSETS[i & 1][slot]) for i in rang...]
    pallas_call x13 -> x10, Pallas kernels: 16.1 us -> 11 us  [call(): pl.pallas_call(kernel, out_shape=outs, in_specs=in_specs or [VM] * len(in...]
  transfers between devices with their start and end apart: 10 -> 9, of which waited for: 5 -> 7; matrix products, arithmetic and copies ran while one was open for 0% -> 0% of each run, Pallas kernels for 28% -> 18%
where the time goes in v2:
time: 31.3 us; the launch traced here: 31.1 us
  starting transfers between devices  11.2 us (36%)
  Pallas kernels  11 us (35%)
  waiting for transfers between devices  8.83 us (28%)
    ppermute x9, starting transfers between devices, swap(): lax.ppermute(x, 'block', [(i, i ^ distance) for i in range(devices_n)])  11.2 us
    pallas_call x10, Pallas kernels, call(): pl.pallas_call(kernel, out_shape=outs, in_specs=in_specs or [VM] * len(in...  11 us
    ppermute x9, waiting for transfers between devices, swap(): lax.ppermute(x, 'block', [(i, i ^ distance) for i in range(devices_n)])  8.83 us
  transfers between devices with their start and end apart: 9, of which 7 were waited for; matrix products, arithmetic and copies ran while one was open for 0% of the time, Pallas kernels for 18%

profile of v2, /device:TPU:0, one launch (start us, length us, event | category | flops | bytes accessed | tf_op | source)
XLA Modules:
  0.0 31.1 jit_solution(607634559577815990)
XLA Ops:
  0.0 3.1 %shard_map.37 = (bf16[8,1536,128]{2,1,0:T(8,128)(2,1)S(1)}, bf16[8,1536,128]{2,1,0:T(8,128)(2,1)S(1)}, bf16[4,1536,128]{2,1,0:T(8,128)(2,1)S(1)}, f32[4,1536,128...) custom-call(bf16[1536,1024]{1,0:T(8,128)(2,1)} %k_hbm.1, bf16[1536,1024]{1,0:T(8,128)(2,1)} %v_hbm.1), custom_call_target="tpu_custom_call" | custom-call | flops 201326592 | bytes 8388608 | tf_op jit(solution)/shard_map/pallas_call | solution.py:230
  3.1 0.6 %collective-permute-start = (f32[4,136,128]{2,1,0:T(8,128)S(1)}, f32[4,136,128]{2,1,0:T(8,128)S(1)}, u32[]{:S(2)}, u32[]{:S(2)}) collective-permute-start(f32[4,136,128]{2,1,0:T(8,128)S(1)} %get-tuple-element.43), channel_id=1, source_target_pairs={{0,1},{1,0},{2,3},{3,2},{4,5},{5,4},{6,7},{7,6},{8,9},{9,8},{10,11... | collective-permute-start | bytes 835592 | tf_op jit(solution)/shard_map/ppermute | solution.py:244
  3.7 0.0 copy-start
  3.7 1.3 %shard_map.39 = (bf16[4,1536,128]{2,1,0:T(8,128)(2,1)S(1)}, f32[4,1536,128]{2,1,0:T(8,128)S(1)}, f32[4,16,128]{2,1,0:T(8,128)S(1)}, f32[4,136,128]{2,1,0:T(8,128)S(1)}) custom-call(bf16[8,1536,128]{2,1,0:T(8,128)(2,1)S(1)} %get-tuple-element.41.k_ref, bf16[8,1536,128]{2,1,0:T(8,128)(2,1)S(1)} %get-tuple-element.40.v_ref), custom_call_target="tpu_custom_call" | custom-call | flops 201326592 | bytes 8388608 | tf_op jit(solution)/shard_map/pallas_call | solution.py:230
  5.0 0.0 collective-permute-done.got_ref
  5.0 2.8 %collective-permute-start.1 = (f32[136,128]{1,0:T(8,128)S(1)}, f32[136,128]{1,0:T(8,128)S(1)}, u32[]{:S(2)}, u32[]{:S(2)}) collective-permute-start(f32[136,128]{1,0:T(8,128)S(1)} %get-tuple-element.45), channel_id=1, source_target_pairs={{0,2},{1,3},{2,0},{3,1},{4,6},{5,7},{6,4},{7,5},{8,10},{9,11},{10,... | collective-permute-start | bytes 208904 | tf_op jit(solution)/shard_map/ppermute | solution.py:244
  7.8 1.6 %collective-permute-start.2 = (f32[136,128]{1,0:T(8,128)S(1)}, f32[136,128]{1,0:T(8,128)S(1)}, u32[]{:S(2)}, u32[]{:S(2)}) collective-permute-start(f32[136,128]{1,0:T(8,128)S(1)} %get-tuple-element.46), channel_id=1, source_target_pairs={{0,4},{1,5},{2,6},{3,7},{4,0},{5,1},{6,2},{7,3},{8,12},{9,13},{10,... | collective-permute-start | bytes 208904 | tf_op jit(solution)/shard_map/ppermute | solution.py:244
  9.4 0.0 collective-permute-start.3
  9.4 0.0 copy-done
  9.4 1.5 %shard_map.41 = (bf16[4,1536,256]{2,1,0:T(8,128)(2,1)S(1)}, f32[4,1536,128]{2,1,0:T(8,128)S(1)}, f32[8,128]{1,0:T(8,128)S(1)}) custom-call(bf16[1536,1024]{1,0:T(8,128)(2,1)S(1)} %copy-done, bf16[4,1536,128]{2,1,0:T(8,128)(2,1)S(1)} %get-tuple-element.48.fk_ref, f32[4,16,128]{2,1,0:T(8,128)S(1)} %get-tuple-element.49.nf_ref), custom_call_target="tpu_custom_call" | custom-call | flops 201326592 | bytes 8388608 | tf_op jit(solution)/shard_map/pallas_call | solution.py:230
  10.9 0.0 collective-permute-done.1.p1
  10.9 1.6 %collective-permute-done.2.p2 = f32[136,128]{1,0:T(8,128)S(1)} collective-permute-done((f32[136,128]{1,0:T(8,128)S(1)}, f32[136,128]{1,0:T(8,128)S(1)}, u32[]{:S(2)}, u32[]{:S(2)}) %collective-permute-start.2) | collective-permute-done | bytes 69664 | tf_op jit(solution)/shard_map/ppermute | solution.py:244
  12.6 2.0 %collective-permute-done.3.p3 = f32[136,128]{1,0:T(8,128)S(1)} collective-permute-done((f32[136,128]{1,0:T(8,128)S(1)}, f32[136,128]{1,0:T(8,128)S(1)}, u32[]{:S(2)}, u32[]{:S(2)}) %collective-permute-start.3) | collective-permute-done | bytes 69664 | tf_op jit(solution)/shard_map/ppermute | solution.py:244
  14.6 0.1 shard_map.42
  14.6 2.7 %collective-permute-start.4 = (f32[136,128]{1,0:T(8,128)S(1)}, f32[136,128]{1,0:T(8,128)S(1)}, u32[]{:S(2)}, u32[]{:S(2)}) collective-permute-start(f32[136,128]{1,0:T(8,128)S(1)} %get-tuple-element.55.total_ref), channel_id=1, source_target_pairs={{0,8},{1,9},{2,10},{3,11},{4,12},{5,13},{6,14},{7,15},{8,0},{9,1},... | collective-permute-start | bytes 208904 | tf_op jit(solution)/shard_map/ppermute | solution.py:244
  17.3 1.5 %shard_map.38 = (bf16[4,1536,256]{2,1,0:T(8,128)(2,1)S(1)}, f32[4,1536,128]{2,1,0:T(8,128)S(1)}, f32[8,128]{1,0:T(8,128)S(1)}) custom-call(bf16[1536,1024]{1,0:T(8,128)(2,1)S(1)} %copy-done, bf16[4,1536,128]{2,1,0:T(8,128)(2,1)S(1)} %get-tuple-element.36.fk_ref, f32[4,16,128]{2,1,0:T(8,128)S(1)} %get-tuple-element.37.nf_ref), custom_call_target="tpu_custom_call" | custom-call | flops 201326592 | bytes 8388608 | tf_op jit(solution)/shard_map/pallas_call | solution.py:230
  18.8 1.8 %collective-permute-done.4.got_ref = f32[136,128]{1,0:T(8,128)S(1)} collective-permute-done((f32[136,128]{1,0:T(8,128)S(1)}, f32[136,128]{1,0:T(8,128)S(1)}, u32[]{:S(2)}, u32[]{:S(2)}) %collective-permute-start.4) | collective-permute-done | bytes 69664 | tf_op jit(solution)/shard_map/ppermute | solution.py:244
  20.7 0.1 collective-permute-start.5
  20.8 1.1 %collective-permute-start.6 = (f32[136,128]{1,0:T(8,128)S(1)}, f32[136,128]{1,0:T(8,128)S(1)}, u32[]{:S(2)}, u32[]{:S(2)}) collective-permute-start(f32[136,128]{1,0:T(8,128)S(1)} %get-tuple-element.59), channel_id=1, source_target_pairs={{0,4},{1,5},{2,6},{3,7},{4,0},{5,1},{6,2},{7,3},{8,12},{9,13},{10,... | collective-permute-start | bytes 208904 | tf_op jit(solution)/shard_map/ppermute | solution.py:244
  21.9 2.4 %collective-permute-start.7 = (f32[136,128]{1,0:T(8,128)S(1)}, f32[136,128]{1,0:T(8,128)S(1)}, u32[]{:S(2)}, u32[]{:S(2)}) collective-permute-start(f32[136,128]{1,0:T(8,128)S(1)} %get-tuple-element.60), channel_id=1, source_target_pairs={{0,6},{1,7},{2,4},{3,5},{4,2},{5,3},{6,0},{7,1},{8,14},{9,15},{10,... | collective-permute-start | bytes 208904 | tf_op jit(solution)/shard_map/ppermute | solution.py:244
  24.3 0.8 %collective-permute-done.5.b1 = f32[136,128]{1,0:T(8,128)S(1)} collective-permute-done((f32[136,128]{1,0:T(8,128)S(1)}, f32[136,128]{1,0:T(8,128)S(1)}, u32[]{:S(2)}, u32[]{:S(2)}) %collective-permute-start.5) | collective-permute-done | bytes 69664 | tf_op jit(solution)/shard_map/ppermute | solution.py:244
  25.1 0.1 collective-permute-done.6.b2
  25.2 2.1 %collective-permute-done.7.b3 = f32[136,128]{1,0:T(8,128)S(1)} collective-permute-done((f32[136,128]{1,0:T(8,128)S(1)}, f32[136,128]{1,0:T(8,128)S(1)}, u32[]{:S(2)}, u32[]{:S(2)}) %collective-permute-start.7) | collective-permute-done | bytes 69664 | tf_op jit(solution)/shard_map/ppermute | solution.py:244
  27.3 0.1 shard_map.44
  27.4 0.1 collective-permute-start.8
  27.5 1.2 %shard_map.45.mine_ref = bf16[1536,512]{1,0:T(8,128)(2,1)S(1)} custom-call(bf16[4,1536,256]{2,1,0:T(8,128)(2,1)S(1)} %get-tuple-element.63.fqs_ref, f32[4,1536,128]{2,1,0:T(8,128)S(1)} %get-tuple-element.64.den_ref, bf16[8,1536,128]{2,1,0:T(8,128)(2,1)S(1)} %get-tuple-element.40.v_ref, f32[4,136,128]{2,1,0:T(8,128)S(1)} %get-tuple-element.65.b_ref, ...), custom_call_target="tpu_custom_call" | custom-call | flops 201326592 | bytes 8388608 | tf_op jit(solution)/shard_map/pallas_call | solution.py:230
  28.7 0.3 collective-permute-done.8.b_ref
  29.0 2.1 %shard_map.46 = bf16[1536,1024]{1,0:T(8,128)(2,1)} custom-call(bf16[4,1536,256]{2,1,0:T(8,128)(2,1)S(1)} %get-tuple-element.38.fqs_ref, f32[4,1536,128]{2,1,0:T(8,128)S(1)} %get-tuple-element.39.den_ref, bf16[8,1536,128]{2,1,0:T(8,128)(2,1)S(1)} %get-tuple-element.40.v_ref, f32[4,136,128]{2,1,0:T(8,128)S(1)} %collective-permute-done.8.b_ref, ...), custom_call_target="tpu_custom_call" | custom-call | flops 201326592 | bytes 8388608 | tf_op jit(solution)/shard_map/pallas_call | solution.py:230
  (2 shorter events, 0.1 us)
Async XLA Ops:
  3.1 1.9 %collective-permute-start = (f32[4,136,128]{2,1,0:T(8,128)S(1)}, f32[4,136,128]{2,1,0:T(8,128)S(1)}, u32[]{:S(2)}, u32[]{:S(2)}) collective-permute-start(f32[4,136,128]{2,1,0:T(8,128)S(1)} %get-tuple-element.43), channel_id=1, source_target_pairs={{0,1},{1,0},{2,3},{3,2},{4,5},{5,4},{6,7},{7,6},{8,9},{9,8},{10,11... | collective-permute-start | bytes 835592 | tf_op jit(solution)/shard_map/ppermute | solution.py:244
  3.7 5.7 %copy-start = (bf16[1536,1024]{1,0:T(8,128)(2,1)S(1)}, bf16[1536,1024]{1,0:T(8,128)(2,1)}, u32[]{:S(2)}) copy-start(bf16[1536,1024]{1,0:T(8,128)(2,1)} %q_ref.3) | copy-start | bytes 9437188
  5.0 5.9 %collective-permute-start.1 = (f32[136,128]{1,0:T(8,128)S(1)}, f32[136,128]{1,0:T(8,128)S(1)}, u32[]{:S(2)}, u32[]{:S(2)}) collective-permute-start(f32[136,128]{1,0:T(8,128)S(1)} %get-tuple-element.45), channel_id=1, source_target_pairs={{0,2},{1,3},{2,0},{3,1},{4,6},{5,7},{6,4},{7,5},{8,10},{9,11},{10,... | collective-permute-start | bytes 208904 | tf_op jit(solution)/shard_map/ppermute | solution.py:244
  7.8 4.8 %collective-permute-start.2 = (f32[136,128]{1,0:T(8,128)S(1)}, f32[136,128]{1,0:T(8,128)S(1)}, u32[]{:S(2)}, u32[]{:S(2)}) collective-permute-start(f32[136,128]{1,0:T(8,128)S(1)} %get-tuple-element.46), channel_id=1, source_target_pairs={{0,4},{1,5},{2,6},{3,7},{4,0},{5,1},{6,2},{7,3},{8,12},{9,13},{10,... | collective-permute-start | bytes 208904 | tf_op jit(solution)/shard_map/ppermute | solution.py:244
  9.4 5.2 %collective-permute-start.3 = (f32[136,128]{1,0:T(8,128)S(1)}, f32[136,128]{1,0:T(8,128)S(1)}, u32[]{:S(2)}, u32[]{:S(2)}) collective-permute-start(f32[136,128]{1,0:T(8,128)S(1)} %get-tuple-element.47), channel_id=1, source_target_pairs={{0,6},{1,7},{2,4},{3,5},{4,2},{5,3},{6,0},{7,1},{8,14},{9,15},{10,... | collective-permute-start | bytes 208904 | tf_op jit(solution)/shard_map/ppermute | solution.py:244
  14.6 6.0 %collective-permute-start.4 = (f32[136,128]{1,0:T(8,128)S(1)}, f32[136,128]{1,0:T(8,128)S(1)}, u32[]{:S(2)}, u32[]{:S(2)}) collective-permute-start(f32[136,128]{1,0:T(8,128)S(1)} %get-tuple-element.55.total_ref), channel_id=1, source_target_pairs={{0,8},{1,9},{2,10},{3,11},{4,12},{5,13},{6,14},{7,15},{8,0},{9,1},... | collective-permute-start | bytes 208904 | tf_op jit(solution)/shard_map/ppermute | solution.py:244
  20.7 4.4 %collective-permute-start.5 = (f32[136,128]{1,0:T(8,128)S(1)}, f32[136,128]{1,0:T(8,128)S(1)}, u32[]{:S(2)}, u32[]{:S(2)}) collective-permute-start(f32[136,128]{1,0:T(8,128)S(1)} %get-tuple-element.58), channel_id=1, source_target_pairs={{0,2},{1,3},{2,0},{3,1},{4,6},{5,7},{6,4},{7,5},{8,10},{9,11},{10,... | collective-permute-start | bytes 208904 | tf_op jit(solution)/shard_map/ppermute | solution.py:244
  20.8 4.4 %collective-permute-start.6 = (f32[136,128]{1,0:T(8,128)S(1)}, f32[136,128]{1,0:T(8,128)S(1)}, u32[]{:S(2)}, u32[]{:S(2)}) collective-permute-start(f32[136,128]{1,0:T(8,128)S(1)} %get-tuple-element.59), channel_id=1, source_target_pairs={{0,4},{1,5},{2,6},{3,7},{4,0},{5,1},{6,2},{7,3},{8,12},{9,13},{10,... | collective-permute-start | bytes 208904 | tf_op jit(solution)/shard_map/ppermute | solution.py:244
  21.9 5.4 %collective-permute-start.7 = (f32[136,128]{1,0:T(8,128)S(1)}, f32[136,128]{1,0:T(8,128)S(1)}, u32[]{:S(2)}, u32[]{:S(2)}) collective-permute-start(f32[136,128]{1,0:T(8,128)S(1)} %get-tuple-element.60), channel_id=1, source_target_pairs={{0,6},{1,7},{2,4},{3,5},{4,2},{5,3},{6,0},{7,1},{8,14},{9,15},{10,... | collective-permute-start | bytes 208904 | tf_op jit(solution)/shard_map/ppermute | solution.py:244
  27.4 1.6 %collective-permute-start.8 = (f32[4,136,128]{2,1,0:T(8,128)S(1)}, f32[4,136,128]{2,1,0:T(8,128)S(1)}, u32[]{:S(2)}, u32[]{:S(2)}) collective-permute-start(f32[4,136,128]{2,1,0:T(8,128)S(1)} %get-tuple-element.61), channel_id=1, source_target_pairs={{0,1},{1,0},{2,3},{3,2},{4,5},{5,4},{6,7},{7,6},{8,9},{9,8},{10,11... | collective-permute-start | bytes 835592 | tf_op jit(solution)/shard_map/ppermute | solution.py:244

commit v3 on v2

--- a/solution.py
+++ b/solution.py
@@ -122,10 +122,10 @@
     return pl.ds(pl.multiple_of((core if mine else 1 - core) * width, width), width)
 
 
-def attend(c, first, fqs_ref, den_ref, v_ref, b_ref, pf_ref, o_ref):
+def attend(c, first, fqs_ref, den_ref, v_ref, b_ref, pf_ref, o_ref, slots=range(HALF)):
     _, local, _ = place()
     rows = pl.ds(c * SPAN, SPAN)
-    for s in range(HALF):
+    for s in slots:
         fqs = fqs_ref[s, rows, :]
         prior = (pf_ref[s, rows, :] + b_ref[s, pl.ds(0, HEAD_DIM), :]).astype(jnp.bfloat16)
         num = jnp.dot(
@@ -143,9 +143,17 @@
         )
 
 
-def post_mine(count, fqs_ref, den_ref, v_ref, b_ref, pf_ref, o_ref):
-    for c in range(count):
-        attend(c, HALF, fqs_ref, den_ref, v_ref, b_ref, pf_ref, o_ref)
+def post_first(count, fqs_ref, den_ref, v_ref, final_ref, got_ref, pf_ref, o_ref, done_ref, b_ref):
+    core, _, _ = place()
+    done_ref[...] = jnp.zeros_like(done_ref)
+    b_ref[0] = final_ref[...] + jnp.where(core == 1, got_ref[0], 0.0)
+    for c in range(count):
+        attend(c, HALF, fqs_ref, den_ref, v_ref, b_ref, pf_ref, o_ref, (0,))
+
+
+def post_mine(count, fqs_ref, den_ref, v_ref, b_ref, pf_ref, first_ref, o_ref):
+    for c in range(count):
+        attend(c, HALF, fqs_ref, den_ref, v_ref, b_ref, pf_ref, o_ref, range(1, HALF))
 
 
 def post_other(count, fqs_ref, den_ref, v_ref, b_ref, pf_ref, mine_ref, o_hbm, o_ref, sems):
@@ -195,7 +203,7 @@
         ref[...] = total_ref[...] + got
 
 
-def both_cores(b0, b1, b2, b3, keep_ref, got_ref, mine_ref, send_ref):
+def both_cores(b0, b1, b2, b3, keep_ref, got_ref, tied, mine_ref, send_ref):
     core, _, _ = place()
     for s, b in enumerate((b0, b1, b2, b3)):
         before = b[...]
@@ -286,16 +294,24 @@
     back = {0: finals[0]}
     for s in SLOT_ORDER:
         back[s] = swap_slot(finals[s], s)
+    half_out = sds((rows, HALF * HEAD_DIM), bf16)
+    first, done_first = call(
+        functools.partial(post_first, count),
+        (fqs_b, den_b, v_vm, finals[0], t_got, pf_b),
+        (half_out, token),
+        scratch_shapes=[pltpu.VMEM((1, PIECE, HEAD_DIM), f32)],
+    )
     four = sds((HALF, PIECE, HEAD_DIM), f32)
     before_b, send_a = small(
-        both_cores, (back[0], back[1], back[2], back[3], t_keep, t_got), (four, four)
+        both_cores, (back[0], back[1], back[2], back[3], t_keep, t_got, done_first), (four, four)
     )
     before_a = swap(send_a, 1)
 
     (mine,) = call(
         functools.partial(post_mine, count),
-        (fqs_b, den_b, v_vm, before_b, pf_b),
-        (sds((rows, HALF * HEAD_DIM), bf16),),
+        (fqs_b, den_b, v_vm, before_b, pf_b, first),
+        (half_out,),
+        input_output_aliases={5: 0},
     )
     return call(
         functools.partial(post_other, count),

time: 31.3 us -> 31.6 us (level)
  Pallas kernels: 11 us -> 11.7 us
  waiting for transfers between devices: 8.83 us -> 8.42 us
    pallas_call x10 -> x11, Pallas kernels: 11 us -> 11.7 us  [call(): pl.pallas_call(kernel, out_shape=outs, in_specs=in_specs or [VM] * len(in...]
    ppermute x9, waiting for transfers between devices: 8.83 us -> 8.42 us  [swap(): lax.ppermute(x, 'block', [(i, i ^ distance) for i in range(devices_n)])]
  transfers between devices with their start and end apart: 9 -> 9, of which waited for: 7 -> 7; matrix products, arithmetic and copies ran while one was open for 0% -> 0% of each run, Pallas kernels for 18% -> 19%
where the time goes in v3:
time: 31.6 us; the launch traced here: 31.4 us
  Pallas kernels  11.7 us (37%)
  starting transfers between devices  11.2 us (35%)
  waiting for transfers between devices  8.42 us (27%)
    pallas_call x11, Pallas kernels, call(): pl.pallas_call(kernel, out_shape=outs, in_specs=in_specs or [VM] * len(in...  11.7 us
    ppermute x9, starting transfers between devices, swap(): lax.ppermute(x, 'block', [(i, i ^ distance) for i in range(devices_n)])  11.2 us
    ppermute x9, waiting for transfers between devices, swap(): lax.ppermute(x, 'block', [(i, i ^ distance) for i in range(devices_n)])  8.42 us
  transfers between devices with their start and end apart: 9, of which 7 were waited for; matrix products, arithmetic and copies ran while one was open for 0% of the time, Pallas kernels for 19%

profile of v3, /device:TPU:0, one launch (start us, length us, event | category | flops | bytes accessed | tf_op | source)
XLA Modules:
  0.0 31.4 jit_solution(1402269605536926568)
XLA Ops:
  0.0 3.1 %shard_map.37 = (bf16[8,1536,128]{2,1,0:T(8,128)(2,1)S(1)}, bf16[8,1536,128]{2,1,0:T(8,128)(2,1)S(1)}, bf16[4,1536,128]{2,1,0:T(8,128)(2,1)S(1)}, f32[4,1536,128...) custom-call(bf16[1536,1024]{1,0:T(8,128)(2,1)} %k_hbm.1, bf16[1536,1024]{1,0:T(8,128)(2,1)} %v_hbm.1), custom_call_target="tpu_custom_call" | custom-call | flops 201326592 | bytes 8388608 | tf_op jit(solution)/shard_map/pallas_call | solution.py:238
  3.1 0.6 %collective-permute-start = (f32[4,136,128]{2,1,0:T(8,128)S(1)}, f32[4,136,128]{2,1,0:T(8,128)S(1)}, u32[]{:S(2)}, u32[]{:S(2)}) collective-permute-start(f32[4,136,128]{2,1,0:T(8,128)S(1)} %get-tuple-element.45), channel_id=1, source_target_pairs={{0,1},{1,0},{2,3},{3,2},{4,5},{5,4},{6,7},{7,6},{8,9},{9,8},{10,11... | collective-permute-start | bytes 835592 | tf_op jit(solution)/shard_map/ppermute | solution.py:252
  3.7 0.0 copy-start
  3.7 1.3 %shard_map.39 = (bf16[4,1536,128]{2,1,0:T(8,128)(2,1)S(1)}, f32[4,1536,128]{2,1,0:T(8,128)S(1)}, f32[4,16,128]{2,1,0:T(8,128)S(1)}, f32[4,136,128]{2,1,0:T(8,128)S(1)}) custom-call(bf16[8,1536,128]{2,1,0:T(8,128)(2,1)S(1)} %get-tuple-element.43.k_ref, bf16[8,1536,128]{2,1,0:T(8,128)(2,1)S(1)} %get-tuple-element.42.v_ref), custom_call_target="tpu_custom_call" | custom-call | flops 201326592 | bytes 8388608 | tf_op jit(solution)/shard_map/pallas_call | solution.py:238
  5.0 0.0 collective-permute-done.got_ref
  5.0 2.8 %collective-permute-start.1 = (f32[136,128]{1,0:T(8,128)S(1)}, f32[136,128]{1,0:T(8,128)S(1)}, u32[]{:S(2)}, u32[]{:S(2)}) collective-permute-start(f32[136,128]{1,0:T(8,128)S(1)} %get-tuple-element.47), channel_id=1, source_target_pairs={{0,2},{1,3},{2,0},{3,1},{4,6},{5,7},{6,4},{7,5},{8,10},{9,11},{10,... | collective-permute-start | bytes 208904 | tf_op jit(solution)/shard_map/ppermute | solution.py:252
  7.8 1.6 %collective-permute-start.2 = (f32[136,128]{1,0:T(8,128)S(1)}, f32[136,128]{1,0:T(8,128)S(1)}, u32[]{:S(2)}, u32[]{:S(2)}) collective-permute-start(f32[136,128]{1,0:T(8,128)S(1)} %get-tuple-element.48), channel_id=1, source_target_pairs={{0,4},{1,5},{2,6},{3,7},{4,0},{5,1},{6,2},{7,3},{8,12},{9,13},{10,... | collective-permute-start | bytes 208904 | tf_op jit(solution)/shard_map/ppermute | solution.py:252
  9.4 0.0 collective-permute-start.3
  9.4 0.0 copy-done
  9.4 1.5 %shard_map.41 = (bf16[4,1536,256]{2,1,0:T(8,128)(2,1)S(1)}, f32[4,1536,128]{2,1,0:T(8,128)S(1)}, f32[8,128]{1,0:T(8,128)S(1)}) custom-call(bf16[1536,1024]{1,0:T(8,128)(2,1)S(1)} %copy-done, bf16[4,1536,128]{2,1,0:T(8,128)(2,1)S(1)} %get-tuple-element.50.fk_ref, f32[4,16,128]{2,1,0:T(8,128)S(1)} %get-tuple-element.51.nf_ref), custom_call_target="tpu_custom_call" | custom-call | flops 201326592 | bytes 8388608 | tf_op jit(solution)/shard_map/pallas_call | solution.py:238
  10.9 0.0 collective-permute-done.1.p1
  10.9 1.6 %collective-permute-done.2.p2 = f32[136,128]{1,0:T(8,128)S(1)} collective-permute-done((f32[136,128]{1,0:T(8,128)S(1)}, f32[136,128]{1,0:T(8,128)S(1)}, u32[]{:S(2)}, u32[]{:S(2)}) %collective-permute-start.2) | collective-permute-done | bytes 69664 | tf_op jit(solution)/shard_map/ppermute | solution.py:252
  12.5 2.0 %collective-permute-done.3.p3 = f32[136,128]{1,0:T(8,128)S(1)} collective-permute-done((f32[136,128]{1,0:T(8,128)S(1)}, f32[136,128]{1,0:T(8,128)S(1)}, u32[]{:S(2)}, u32[]{:S(2)}) %collective-permute-start.3) | collective-permute-done | bytes 69664 | tf_op jit(solution)/shard_map/ppermute | solution.py:252
  14.6 0.1 shard_map.42
  14.6 2.7 %collective-permute-start.4 = (f32[136,128]{1,0:T(8,128)S(1)}, f32[136,128]{1,0:T(8,128)S(1)}, u32[]{:S(2)}, u32[]{:S(2)}) collective-permute-start(f32[136,128]{1,0:T(8,128)S(1)} %get-tuple-element.57.total_ref), channel_id=1, source_target_pairs={{0,8},{1,9},{2,10},{3,11},{4,12},{5,13},{6,14},{7,15},{8,0},{9,1},... | collective-permute-start | bytes 208904 | tf_op jit(solution)/shard_map/ppermute | solution.py:252
  17.3 1.5 %shard_map.38 = (bf16[4,1536,256]{2,1,0:T(8,128)(2,1)S(1)}, f32[4,1536,128]{2,1,0:T(8,128)S(1)}, f32[8,128]{1,0:T(8,128)S(1)}) custom-call(bf16[1536,1024]{1,0:T(8,128)(2,1)S(1)} %copy-done, bf16[4,1536,128]{2,1,0:T(8,128)(2,1)S(1)} %get-tuple-element.38.fk_ref, f32[4,16,128]{2,1,0:T(8,128)S(1)} %get-tuple-element.39.nf_ref), custom_call_target="tpu_custom_call" | custom-call | flops 201326592 | bytes 8388608 | tf_op jit(solution)/shard_map/pallas_call | solution.py:238
  18.8 1.8 %collective-permute-done.4.got_ref = f32[136,128]{1,0:T(8,128)S(1)} collective-permute-done((f32[136,128]{1,0:T(8,128)S(1)}, f32[136,128]{1,0:T(8,128)S(1)}, u32[]{:S(2)}, u32[]{:S(2)}) %collective-permute-start.4) | collective-permute-done | bytes 69664 | tf_op jit(solution)/shard_map/ppermute | solution.py:252
  20.7 0.1 collective-permute-start.5
  20.8 1.1 %collective-permute-start.6 = (f32[136,128]{1,0:T(8,128)S(1)}, f32[136,128]{1,0:T(8,128)S(1)}, u32[]{:S(2)}, u32[]{:S(2)}) collective-permute-start(f32[136,128]{1,0:T(8,128)S(1)} %get-tuple-element.61), channel_id=1, source_target_pairs={{0,4},{1,5},{2,6},{3,7},{4,0},{5,1},{6,2},{7,3},{8,12},{9,13},{10,... | collective-permute-start | bytes 208904 | tf_op jit(solution)/shard_map/ppermute | solution.py:252
  21.9 2.4 %collective-permute-start.7 = (f32[136,128]{1,0:T(8,128)S(1)}, f32[136,128]{1,0:T(8,128)S(1)}, u32[]{:S(2)}, u32[]{:S(2)}) collective-permute-start(f32[136,128]{1,0:T(8,128)S(1)} %get-tuple-element.62), channel_id=1, source_target_pairs={{0,6},{1,7},{2,4},{3,5},{4,2},{5,3},{6,0},{7,1},{8,14},{9,15},{10,... | collective-permute-start | bytes 208904 | tf_op jit(solution)/shard_map/ppermute | solution.py:252
  24.3 0.4 %shard_map.44 = (bf16[1536,512]{1,0:T(8,128)(2,1)S(1)}, f32[8,128]{1,0:T(8,128)S(1)}) custom-call(bf16[4,1536,256]{2,1,0:T(8,128)(2,1)S(1)} %get-tuple-element.63.fqs_ref, f32[4,1536,128]{2,1,0:T(8,128)S(1)} %get-tuple-element.64.den_ref, bf16[8,1536,128]{2,1,0:T(8,128)(2,1)S(1)} %get-tuple-element.42.v_ref, f32[136,128]{1,0:T(8,128)S(1)} %get-tuple-element.59.final_ref.b0, ...), custom_call_target="tpu_custom_call" | custom-call | flops 201326592 | bytes 8388608 | tf_op jit(solution)/shard_map/pallas_call | solution.py:238
  24.7 0.4 %collective-permute-done.5.b1 = f32[136,128]{1,0:T(8,128)S(1)} collective-permute-done((f32[136,128]{1,0:T(8,128)S(1)}, f32[136,128]{1,0:T(8,128)S(1)}, u32[]{:S(2)}, u32[]{:S(2)}) %collective-permute-start.5) | collective-permute-done | bytes 69664 | tf_op jit(solution)/shard_map/ppermute | solution.py:252
  25.1 0.1 collective-permute-done.6.b2
  25.2 2.1 %collective-permute-done.7.b3 = f32[136,128]{1,0:T(8,128)S(1)} collective-permute-done((f32[136,128]{1,0:T(8,128)S(1)}, f32[136,128]{1,0:T(8,128)S(1)}, u32[]{:S(2)}, u32[]{:S(2)}) %collective-permute-start.7) | collective-permute-done | bytes 69664 | tf_op jit(solution)/shard_map/ppermute | solution.py:252
  27.3 0.1 shard_map.45
  27.4 0.1 collective-permute-start.8
  27.5 1.2 %shard_map.46.mine_ref = bf16[1536,512]{1,0:T(8,128)(2,1)S(1)} custom-call(bf16[4,1536,256]{2,1,0:T(8,128)(2,1)S(1)} %get-tuple-element.63.fqs_ref, f32[4,1536,128]{2,1,0:T(8,128)S(1)} %get-tuple-element.64.den_ref, bf16[8,1536,128]{2,1,0:T(8,128)(2,1)S(1)} %get-tuple-element.42.v_ref, ...), custom_call_target="tpu_custom_call", output_to_operand_aliasing={{}: (5, {})} | custom-call | flops 201326592 | bytes 8388608 | tf_op jit(solution)/shard_map/pallas_call | solution.py:238
  28.7 0.3 collective-permute-done.8.b_ref
  29.0 2.4 %shard_map.47 = bf16[1536,1024]{1,0:T(8,128)(2,1)} custom-call(bf16[4,1536,256]{2,1,0:T(8,128)(2,1)S(1)} %get-tuple-element.40.fqs_ref, f32[4,1536,128]{2,1,0:T(8,128)S(1)} %get-tuple-element.41.den_ref, bf16[8,1536,128]{2,1,0:T(8,128)(2,1)S(1)} %get-tuple-element.42.v_ref, f32[4,136,128]{2,1,0:T(8,128)S(1)} %collective-permute-done.8.b_ref, ...), custom_call_target="tpu_custom_call" | custom-call | flops 201326592 | bytes 8388608 | tf_op jit(solution)/shard_map/pallas_call | solution.py:238
  (2 shorter events, 0.1 us)
Async XLA Ops:
  3.1 1.9 %collective-permute-start = (f32[4,136,128]{2,1,0:T(8,128)S(1)}, f32[4,136,128]{2,1,0:T(8,128)S(1)}, u32[]{:S(2)}, u32[]{:S(2)}) collective-permute-start(f32[4,136,128]{2,1,0:T(8,128)S(1)} %get-tuple-element.45), channel_id=1, source_target_pairs={{0,1},{1,0},{2,3},{3,2},{4,5},{5,4},{6,7},{7,6},{8,9},{9,8},{10,11... | collective-permute-start | bytes 835592 | tf_op jit(solution)/shard_map/ppermute | solution.py:252
  3.7 5.7 %copy-start = (bf16[1536,1024]{1,0:T(8,128)(2,1)S(1)}, bf16[1536,1024]{1,0:T(8,128)(2,1)}, u32[]{:S(2)}) copy-start(bf16[1536,1024]{1,0:T(8,128)(2,1)} %q_ref.3) | copy-start | bytes 9437188
  5.0 5.9 %collective-permute-start.1 = (f32[136,128]{1,0:T(8,128)S(1)}, f32[136,128]{1,0:T(8,128)S(1)}, u32[]{:S(2)}, u32[]{:S(2)}) collective-permute-start(f32[136,128]{1,0:T(8,128)S(1)} %get-tuple-element.47), channel_id=1, source_target_pairs={{0,2},{1,3},{2,0},{3,1},{4,6},{5,7},{6,4},{7,5},{8,10},{9,11},{10,... | collective-permute-start | bytes 208904 | tf_op jit(solution)/shard_map/ppermute | solution.py:252
  7.8 4.8 %collective-permute-start.2 = (f32[136,128]{1,0:T(8,128)S(1)}, f32[136,128]{1,0:T(8,128)S(1)}, u32[]{:S(2)}, u32[]{:S(2)}) collective-permute-start(f32[136,128]{1,0:T(8,128)S(1)} %get-tuple-element.48), channel_id=1, source_target_pairs={{0,4},{1,5},{2,6},{3,7},{4,0},{5,1},{6,2},{7,3},{8,12},{9,13},{10,... | collective-permute-start | bytes 208904 | tf_op jit(solution)/shard_map/ppermute | solution.py:252
  9.4 5.2 %collective-permute-start.3 = (f32[136,128]{1,0:T(8,128)S(1)}, f32[136,128]{1,0:T(8,128)S(1)}, u32[]{:S(2)}, u32[]{:S(2)}) collective-permute-start(f32[136,128]{1,0:T(8,128)S(1)} %get-tuple-element.49), channel_id=1, source_target_pairs={{0,6},{1,7},{2,4},{3,5},{4,2},{5,3},{6,0},{7,1},{8,14},{9,15},{10,... | collective-permute-start | bytes 208904 | tf_op jit(solution)/shard_map/ppermute | solution.py:252
  14.6 6.0 %collective-permute-start.4 = (f32[136,128]{1,0:T(8,128)S(1)}, f32[136,128]{1,0:T(8,128)S(1)}, u32[]{:S(2)}, u32[]{:S(2)}) collective-permute-start(f32[136,128]{1,0:T(8,128)S(1)} %get-tuple-element.57.total_ref), channel_id=1, source_target_pairs={{0,8},{1,9},{2,10},{3,11},{4,12},{5,13},{6,14},{7,15},{8,0},{9,1},... | collective-permute-start | bytes 208904 | tf_op jit(solution)/shard_map/ppermute | solution.py:252
  20.7 4.4 %collective-permute-start.5 = (f32[136,128]{1,0:T(8,128)S(1)}, f32[136,128]{1,0:T(8,128)S(1)}, u32[]{:S(2)}, u32[]{:S(2)}) collective-permute-start(f32[136,128]{1,0:T(8,128)S(1)} %get-tuple-element.60), channel_id=1, source_target_pairs={{0,2},{1,3},{2,0},{3,1},{4,6},{5,7},{6,4},{7,5},{8,10},{9,11},{10,... | collective-permute-start | bytes 208904 | tf_op jit(solution)/shard_map/ppermute | solution.py:252
  20.8 4.4 %collective-permute-start.6 = (f32[136,128]{1,0:T(8,128)S(1)}, f32[136,128]{1,0:T(8,128)S(1)}, u32[]{:S(2)}, u32[]{:S(2)}) collective-permute-start(f32[136,128]{1,0:T(8,128)S(1)} %get-tuple-element.61), channel_id=1, source_target_pairs={{0,4},{1,5},{2,6},{3,7},{4,0},{5,1},{6,2},{7,3},{8,12},{9,13},{10,... | collective-permute-start | bytes 208904 | tf_op jit(solution)/shard_map/ppermute | solution.py:252
  21.9 5.4 %collective-permute-start.7 = (f32[136,128]{1,0:T(8,128)S(1)}, f32[136,128]{1,0:T(8,128)S(1)}, u32[]{:S(2)}, u32[]{:S(2)}) collective-permute-start(f32[136,128]{1,0:T(8,128)S(1)} %get-tuple-element.62), channel_id=1, source_target_pairs={{0,6},{1,7},{2,4},{3,5},{4,2},{5,3},{6,0},{7,1},{8,14},{9,15},{10,... | collective-permute-start | bytes 208904 | tf_op jit(solution)/shard_map/ppermute | solution.py:252
  27.4 1.6 %collective-permute-start.8 = (f32[4,136,128]{2,1,0:T(8,128)S(1)}, f32[4,136,128]{2,1,0:T(8,128)S(1)}, u32[]{:S(2)}, u32[]{:S(2)}) collective-permute-start(f32[4,136,128]{2,1,0:T(8,128)S(1)} %get-tuple-element.67), channel_id=1, source_target_pairs={{0,1},{1,0},{2,3},{3,2},{4,5},{5,4},{6,7},{7,6},{8,9},{9,8},{10,11... | collective-permute-start | bytes 835592 | tf_op jit(solution)/shard_map/ppermute | solution.py:252
